TPU v7x, 32 devices: a whole 2x2x4 slice. The times are simulated.
32 devices in a mesh: box: 8 (over z, y), face: 4 (over x, core).
Axes of the slice: x: 2, y: 2, z: 4, core: 2. Of those that a mesh axis runs over, the one named last changes fastest.
Arguments:
- blocks: bfloat16 [32, 24, 24, 128, 128], P('box', 'face'), may hold values from -1 to 2
- pattern: int32 [32, 24, 24], P('box', 'face'), may hold values from 0 to 1, as said below
- shared: int32 [32, 4], P('box'), may hold values from 0 to 23, as said below
- sketch: bfloat16 [3072, 256], replicated, may hold values from -6 to 6
Outputs:
- merged: bfloat16 [32, 3072, 256], P('box', 'face')
Inputs may be any that keep to these rules, and one draw needn't show every extreme that they name: `pattern`: 1 where a block is stored; every diagonal block is stored. `shared`: 4 distinct block indices in increasing order.
All inputs are finite; a program needn't handle non-finite values.
Results may differ from a plain program's by a relative error of at most 0.0085.
Values may be sent and summed in bfloat16 or wider, within the bound.
No kernel may reach another device: no remote copies, remote signals or barrier semaphores. Data moves between devices by JAX's collectives and lax.ppermute only.
A program may use at most 128 MiB of HBM per device.

v0:
```python
import functools

import jax
import jax.numpy as jnp
from jax import lax
from jax.experimental import pallas as pl
from jax.experimental.pallas import tpu as pltpu
from jax.sharding import PartitionSpec as P


ITERS = 4
MIB = 1024 * 1024
SMEM = pl.BlockSpec(memory_space=pltpu.SMEM)
VMEM = pl.BlockSpec(memory_space=pltpu.VMEM)
ANY = pl.BlockSpec(memory_space=pl.ANY)
HBM = pl.BlockSpec(memory_space=pltpu.HBM)


def call(kernel, out_shape, mib, in_specs, out_specs, flops=0, moved=0, **kwargs):
    return pl.pallas_call(
        kernel,
        out_shape=out_shape,
        in_specs=in_specs,
        out_specs=out_specs,
        compiler_params=pltpu.CompilerParams(vmem_limit_bytes=mib * MIB),
        cost_estimate=pl.CostEstimate(flops=flops, bytes_accessed=moved, transcendentals=0),
        **kwargs,
    )


def place():
    face, box = lax.axis_index("face"), lax.axis_index("box")
    return lax.rem(face, 2), lax.bitwise_or(lax.shift_left(lax.div(face, 2), 1), lax.rem(box, 2))


def box_at(distance, boxes):
    return lax.rem(lax.bitwise_xor(place()[1], distance), boxes)


def gather_kernel(shared, pattern_hbm, blocks, send, keep, pattern, sems):
    boxes, half, blk, width = keep.shape
    row_count = blocks.shape[1]
    slots = 2 * half
    row_start = lax.axis_index("face") * row_count
    core = place()[0]
    last = boxes * slots * slots

    def each(action):
        for order, (where, target) in enumerate(((1 - core, send), (core, keep))):
            for box in range(boxes):
                for part in range(half):
                    slot = where * half + part
                    row = shared[box, slot] - row_start
                    owned = jnp.logical_and(row >= 0, row < row_count)
                    first = ((order * boxes + box) * half + part) * slots
                    action(box, row, owned, first, target, part)

    def copy(box, row, first, target, part, other):
        return pltpu.make_async_copy(
            blocks.at[box, row, shared[box, other]],
            target.at[box, part, :, pl.ds(other * blk, blk)],
            sems.at[first + other],
        )

    def start(box, row, owned, first, target, part):
        @pl.when(owned)
        def _():
            for other in range(slots):
                copy(box, row, first, target, part, other).start()

    def clear(box, row, owned, first, target, part):
        @pl.when(jnp.logical_not(owned))
        def _():
            target[box, part] = jnp.zeros((blk, width), target.dtype)

    def finish(box, row, owned, first, target, part):
        @pl.when(owned)
        def _():
            for other in range(slots):
                copy(box, row, first, target, part, other).wait()

                @pl.when(pattern[row, box, shared[box, other]] == 0)
                def _():
                    target[box, part, :, pl.ds(other * blk, blk)] = jnp.zeros((blk, blk), target.dtype)

    to_scalars = pltpu.make_async_copy(pattern_hbm, pattern, sems.at[last])
    to_scalars.start()
    each(start)
    each(clear)
    to_scalars.wait()
    each(finish)


def merge_kernel(keep, received, *outs):
    for distance, out in enumerate(outs):
        pair = box_at(distance, keep.shape[0])
        out[...] = keep[pair] + received[pair]


def side_sum_kernel(*refs):
    ins, out = refs[:-2], refs[-1]
    for side in range(2):
        total = ins[side][...]
        for ref in ins[side + 2 :: 2]:
            total = total + ref[...]
        out[side] = total


def system_kernel(mine, theirs, system, diag_sum):
    _, half, blk, width = mine.shape
    slots = 2 * half
    core = place()[0]
    for part, where in ((mine, core), (theirs, 1 - core)):
        for side in range(2):
            rows = pl.ds(pl.multiple_of(where * half * blk, half * blk), half * blk)
            system[rows, side * width : (side + 1) * width] = part[side].reshape(half * blk, width)
    eye = lax.broadcasted_iota(jnp.int32, (blk, blk), 0) == lax.broadcasted_iota(jnp.int32, (blk, blk), 1)
    for slot in range(slots):
        rows = slice(slot * blk, (slot + 1) * blk)
        both = system[rows, rows].astype(jnp.float32) + system[
            rows, width + slot * blk : width + (slot + 1) * blk
        ].astype(jnp.float32)
        line = jnp.sum(jnp.where(eye, both, 0.0), axis=1, keepdims=True)
        diag_sum[rows, :] = jnp.broadcast_to(line, (blk, diag_sum.shape[1]))


def masked_row(mask, blocks, box, row):
    parts = [
        blocks[box, row, column] * mask[box, row, column : column + 1] for column in range(blocks.shape[2])
    ]
    return jnp.concatenate(parts, axis=1)


def right_kernel(shared, mask, blocks, sketch, send, keep):
    boxes, row_count = blocks.shape[:2]
    slots, half_cols = keep.shape[1], keep.shape[3]
    row_start = lax.axis_index("face") * row_count
    core = place()[0]

    def one(step, carry):
        box, slot = step // slots, lax.rem(step, slots)
        row = shared[box, slot] - row_start
        owned = jnp.logical_and(row >= 0, row < row_count)

        @pl.when(owned)
        def _():
            left = masked_row(mask, blocks, box, row)
            product = jnp.dot(left, sketch[...], preferred_element_type=jnp.float32).astype(keep.dtype)
            low, high = product[:, :half_cols], product[:, half_cols:]
            keep[box, slot] = jnp.where(core == 0, low, high)
            send[box, slot] = jnp.where(core == 0, high, low)

        @pl.when(jnp.logical_not(owned))
        def _():
            keep[box, slot] = jnp.zeros(keep.shape[2:], keep.dtype)
            send[box, slot] = jnp.zeros(send.shape[2:], send.dtype)

        return carry

    lax.fori_loop(0, boxes * slots, one, 0)


def sketch_kernel(distance, mask, blocks, sketch, sketched):
    boxes, row_count, _, blk, _ = blocks.shape
    box = box_at(distance, boxes)
    for row in range(row_count):
        left = masked_row(mask, blocks, box, row)
        product = jnp.dot(left, sketch[...], preferred_element_type=jnp.float32)
        sketched[row * blk : (row + 1) * blk] = product.astype(sketched.dtype)


def side_kernel(shared, pattern, blocks, order_only, *sides):
    del order_only
    boxes, row_count, _, blk, _ = blocks.shape
    for distance, side in enumerate(sides):
        box = box_at(distance, boxes)
        for slot in range(shared.shape[1]):
            column = shared[box, slot]
            for row in range(row_count):
                stored = jnp.where(pattern[row, box, column] != 0, 1.0, 0.0).astype(blocks.dtype)
                side[row * blk : (row + 1) * blk, slot * blk : (slot + 1) * blk] = (
                    blocks[box, row, column] * stored
                )


def solve_kernel(system, diag_sum, *refs):
    rhs_refs, out = refs[:-1], refs[-1]
    right_side = rhs_refs[0][...].astype(jnp.float32)
    for ref in rhs_refs[1:]:
        right_side = right_side + ref[...].astype(jnp.float32)
    slots, blk, cols = right_side.shape
    right_side = right_side.reshape(slots * blk, cols)
    potential = right_side / diag_sum[...]
    for _ in range(ITERS - 1):
        high = potential.astype(jnp.bfloat16)
        low = (potential - high.astype(jnp.float32)).astype(jnp.bfloat16)
        both = jnp.concatenate([high, low], axis=1)
        stacked = jnp.concatenate([both, both], axis=0)
        applied = jnp.dot(system[...], stacked, preferred_element_type=jnp.float32)
        applied = applied[:, :cols] + applied[:, cols:]
        potential = potential + (right_side - applied) / diag_sum[...]
    out[...] = potential.astype(out.dtype).reshape(out.shape)


def correct_kernel(distance, sketched, side, mine, theirs, *refs):
    out, result, sems = refs[-3:]
    boxes = out.shape[0]
    slots, blk, cols = mine.shape
    order = sketched.shape[0]
    pieces = sems.shape[0]
    core = place()[0]
    box = box_at(distance, boxes)
    own = mine[...].reshape(slots * blk, cols)
    other = theirs[...].reshape(slots * blk, cols)
    parts = [jnp.where(core == 0, own, other), jnp.where(core == 0, other, own)]
    potential = jnp.concatenate(parts, axis=1)
    copies = []
    for piece in range(pieces):
        rows = pl.ds(piece * (order // pieces), order // pieces)
        correction = jnp.dot(side[rows], potential, preferred_element_type=jnp.float32)
        result[rows] = (sketched[rows].astype(jnp.float32) - correction).astype(result.dtype)
        copy = pltpu.make_async_copy(result.at[rows], out.at[box, rows], sems.at[piece])
        copy.start()
        copies.append(copy)
    for copy in copies:
        copy.wait()


def local(blocks, pattern, shared, sketch):
    boxes, row_count, all_blocks, blk, _ = blocks.shape
    slots = shared.shape[1]
    half = slots // 2
    cols = sketch.shape[1]
    box_size, face_size = lax.axis_size("box"), lax.axis_size("face")
    chips = face_size
    kind = blocks.dtype
    by_row = jnp.transpose(pattern, (1, 0, 2))
    outside = jnp.all(shared[:, :, None] != lax.iota(jnp.int32, all_blocks)[None, None, :], axis=1)
    mask = jnp.logical_and(pattern != 0, outside[:, None, :]).astype(kind)
    mask = jnp.broadcast_to(mask[..., None], (boxes, row_count, all_blocks, blk))

    def other_core(value):
        pairs = [(f, f ^ 1) for f in range(face_size)]
        return lax.ppermute(value, "face", pairs)

    def chip_at(value, distance):
        pairs = []
        for b in range(box_size):
            for f in range(face_size):
                target = (b ^ (distance & 1)) * face_size + (f ^ (2 * (distance >> 1)))
                pairs.append((b * face_size + f, target))
        return lax.ppermute(value, ("box", "face"), pairs)

    def around(values):
        return [values[0]] + [chip_at(values[d], d) for d in range(1, len(values))]

    def merged(keep, received):
        shape = jax.ShapeDtypeStruct(keep.shape[1:], kind)
        return call(
            merge_kernel, [shape] * chips, 6,
            [VMEM, VMEM], [VMEM] * chips, moved=4 * keep.size * 2,
        )(keep, received)

    part_shape = jax.ShapeDtypeStruct((boxes, half, blk, slots * blk), kind)
    in_place = lambda value: pltpu.with_memory_space_constraint(value, pltpu.HBM)
    send, keep = call(
        gather_kernel, [part_shape] * 2, 4,
        [SMEM, HBM, HBM], [VMEM, VMEM], moved=2 * MIB,
        scratch_shapes=[
            pltpu.SMEM(by_row.shape, jnp.int32),
            pltpu.SemaphoreType.DMA((boxes * slots * slots + 1,)),
        ],
    )(in_place(shared), in_place(by_row), in_place(blocks))
    outs = merged(keep, other_core(send))
    arrived = around(outs)

    order = row_count * blk
    half_shape = jax.ShapeDtypeStruct((boxes, slots, blk, cols // 2), kind)
    send_y, keep_y = call(
        right_kernel, [half_shape] * 2, 6, [SMEM] + [VMEM] * 3, [VMEM] * 2,
        flops=2 * slots * blk * all_blocks * blk * cols, moved=4 * MIB,
    )(shared, mask, blocks, sketch)
    sketches = [
        call(
            functools.partial(sketch_kernel, distance),
            jax.ShapeDtypeStruct((order, cols), kind), 6, [VMEM] * 3, VMEM,
            flops=2 * order * all_blocks * blk * cols, moved=6 * MIB,
        )(mask, blocks, sketch)
        for distance in range(boxes)
    ]
    outs_y = merged(keep_y, other_core(send_y))
    arrived_y = around(outs_y)

    both_shape = jax.ShapeDtypeStruct((2,) + outs[0].shape, kind)
    mine = call(
        side_sum_kernel, both_shape, 4, [VMEM] * chips + [ANY], VMEM, moved=3 * MIB // 2
    )(*arrived, outs_y[0])
    system, diag_sum = call(
        system_kernel,
        [
            jax.ShapeDtypeStruct((slots * blk, 2 * slots * blk), kind),
            jax.ShapeDtypeStruct((slots * blk, cols // 2), jnp.float32),
        ],
        4, [VMEM, VMEM], [VMEM, VMEM], moved=2 * MIB,
    )(mine, other_core(mine))

    sides = call(
        side_kernel, [jax.ShapeDtypeStruct((order, slots * blk), kind)] * boxes, 6,
        [SMEM, SMEM, VMEM, ANY], [VMEM] * boxes, moved=6 * MIB,
    )(shared, by_row, blocks, sketches[-1])

    potential = call(
        solve_kernel,
        jax.ShapeDtypeStruct((slots, blk, cols // 2), kind), 8,
        [VMEM] * (2 + chips), VMEM,
        flops=2 * (ITERS - 1) * 2 * (slots * blk) ** 2 * cols, moved=2 * MIB,
    )(system, diag_sum, *arrived_y)

    back = around([potential] * boxes)
    out_shape = jax.ShapeDtypeStruct((boxes, order, cols), kind)
    results = []
    for distance, mine in enumerate(back):
        if distance == 1 or distance >= 3:
            earlier = 0 if distance == 1 else distance - 2
            mine, results[earlier] = lax.optimization_barrier((mine, results[earlier]))
        result = results[-1] if results else None
        corrected = call(
            functools.partial(correct_kernel, distance), out_shape, 4,
            [VMEM] * 4 + ([] if result is None else [HBM]), HBM,
            flops=2 * order * slots * blk * cols, moved=2 * MIB,
            scratch_shapes=[pltpu.VMEM((order, cols), kind), pltpu.SemaphoreType.DMA((3,))],
            input_output_aliases={} if result is None else {4: 0},
        )(sketches[distance], sides[distance], mine, other_core(mine), *([] if result is None else [result]))
        results.append(corrected)
    return results[-1]


def solution(mesh):
    return jax.shard_map(
        local,
        mesh=mesh,
        in_specs=(P("box", "face", None, None, None), P("box", "face", None), P("box", None), P()),
        out_specs=P("box", "face", None),
        check_vma=False,
    )
```

profile of v0, /device:TPU:0, one launch (start us, length us, event | category | flops | bytes accessed | tf_op | source)
XLA Modules:
  0.0 60.0 jit_solution(14173291103140792955)
XLA Ops:
  0.0 2.9 %shard_map.48 = (bf16[4,2,128,512]{3,2,1,0:T(8,128)(2,1)S(1)}, bf16[4,2,128,512]{3,2,1,0:T(8,128)(2,1)S(1)}) custom-call(s32[4,4]{1,0:T(4,128)} %shared.5, s32[6,4,24]{2,1,0:T(4,128)} %bitcast.1, bf16[4,6,24,128,128]{4,3,2,1,0:T(8,128)(2,1)} %blocks.13), custom_call_target="tpu_custom_call" | custom-call | bytes 2097152 | tf_op jit(solution)/shard_map/pallas_call | solution.py:266
  3.0 0.5 collective-permute-start
  3.4 0.1 fusion
  3.5 0.1 broadcast_in_dim.2.mask
  3.7 3.0 %copy-done = bf16[4,6,24,128,128]{4,3,2,1,0:T(8,128)(2,1)S(1)} copy-done((bf16[4,6,24,128,128]{4,3,2,1,0:T(8,128)(2,1)S(1)}, bf16[4,6,24,128,128]{4,3,2,1,0:T(8,128)(2,1)}, u32[]{:S(2)}) %copy-start) | copy-done | bytes 18874392
  6.7 1.4 %copy-done.1 = bf16[3072,256]{1,0:T(8,128)(2,1)S(1)} copy-done((bf16[3072,256]{1,0:T(8,128)(2,1)S(1)}, bf16[3072,256]{1,0:T(8,128)(2,1)}, u32[]{:S(2)}) %copy-start.1) | copy-done | bytes 1572888
  8.1 2.6 %shard_map.50 = (bf16[4,4,128,128]{3,2,1,0:T(8,128)(2,1)S(1)}, bf16[4,4,128,128]{3,2,1,0:T(8,128)(2,1)S(1)}) custom-call(s32[4,4]{1,0:T(4,128)S(1)} %copy-done.4, bf16[4,6,24,128]{3,2,1,0:T(8,128)(2,1)S(1)} %broadcast_in_dim.2.mask, bf16[4,6,24,128,128]{4,3,2,1,0:T(8,128)(2,1)S(1)} %copy-done, bf16[3072,256]{1,0:T(8,128)(2,1)S(1)} %copy-done.1), custom_call_target="tpu_custom_call" | custom-call | flops 805306368 | bytes 4194304 | tf_op jit(solution)/shard_map/pallas_call | solution.py:279
  10.6 0.1 collective-permute-start.4
  10.8 0.0 collective-permute-done.received
  10.8 0.1 shard_map.49
  10.9 2.6 %collective-permute-start.1 = (bf16[2,128,512]{2,1,0:T(8,128)(2,1)S(1)}, bf16[2,128,512]{2,1,0:T(8,128)(2,1)S(1)}, u32[]{:S(2)}, u32[]{:S(2)}) collective-permute-start(bf16[2,128,512]{2,1,0:T(8,128)(2,1)S(1)} %get-tuple-element.30), channel_id=1, source_target_pairs={{0,4},{1,5},{2,6},{3,7},{4,0},{5,1},{6,2},{7,3},{8,12},{9,13},{10,... | collective-permute-start | bytes 786440 | tf_op jit(solution)/shard_map/ppermute | solution.py:252
  13.5 3.1 %collective-permute-start.2 = (bf16[2,128,512]{2,1,0:T(8,128)(2,1)S(1)}, bf16[2,128,512]{2,1,0:T(8,128)(2,1)S(1)}, u32[]{:S(2)}, u32[]{:S(2)}) collective-permute-start(bf16[2,128,512]{2,1,0:T(8,128)(2,1)S(1)} %get-tuple-element.31), channel_id=1, source_target_pairs={{0,2},{1,3},{2,0},{3,1},{4,6},{5,7},{6,4},{7,5},{8,10},{9,11},{10,... | collective-permute-start | bytes 786440 | tf_op jit(solution)/shard_map/ppermute | solution.py:252
  16.6 0.0 collective-permute-start.3
  16.6 0.0 collective-permute-done.4.received
  16.6 0.1 shard_map.51
  16.7 3.7 %collective-permute-done.1.refs_1_ = bf16[2,128,512]{2,1,0:T(8,128)(2,1)S(1)} collective-permute-done((bf16[2,128,512]{2,1,0:T(8,128)(2,1)S(1)}, bf16[2,128,512]{2,1,0:T(8,128)(2,1)S(1)}, u32[]{:S(2)}, u32[]{:S(2)}) %collective-permute-start.1) | collective-permute-done | bytes 262176 | tf_op jit(solution)/shard_map/ppermute | solution.py:252
  20.4 3.4 %collective-permute-done.2.refs_2_ = bf16[2,128,512]{2,1,0:T(8,128)(2,1)S(1)} collective-permute-done((bf16[2,128,512]{2,1,0:T(8,128)(2,1)S(1)}, bf16[2,128,512]{2,1,0:T(8,128)(2,1)S(1)}, u32[]{:S(2)}, u32[]{:S(2)}) %collective-permute-start.2) | collective-permute-done | bytes 262176 | tf_op jit(solution)/shard_map/ppermute | solution.py:252
  23.8 4.9 %collective-permute-done.3.refs_3_ = bf16[2,128,512]{2,1,0:T(8,128)(2,1)S(1)} collective-permute-done((bf16[2,128,512]{2,1,0:T(8,128)(2,1)S(1)}, bf16[2,128,512]{2,1,0:T(8,128)(2,1)S(1)}, u32[]{:S(2)}, u32[]{:S(2)}) %collective-permute-start.3) | collective-permute-done | bytes 262176 | tf_op jit(solution)/shard_map/ppermute | solution.py:252
  28.7 0.1 shard_map.52.mine
  28.8 0.1 collective-permute-start.5
  28.8 1.7 %collective-permute-start.6 = (bf16[4,128,128]{2,1,0:T(8,128)(2,1)S(1)}, bf16[4,128,128]{2,1,0:T(8,128)(2,1)S(1)}, u32[]{:S(2)}, u32[]{:S(2)}) collective-permute-start(bf16[4,128,128]{2,1,0:T(8,128)(2,1)S(1)} %get-tuple-element.38), channel_id=1, source_target_pairs={{0,4},{1,5},{2,6},{3,7},{4,0},{5,1},{6,2},{7,3},{8,12},{9,13},{10,... | collective-permute-start | bytes 393224 | tf_op jit(solution)/shard_map/ppermute | solution.py:252
  30.6 1.7 %collective-permute-start.7 = (bf16[4,128,128]{2,1,0:T(8,128)(2,1)S(1)}, bf16[4,128,128]{2,1,0:T(8,128)(2,1)S(1)}, u32[]{:S(2)}, u32[]{:S(2)}) collective-permute-start(bf16[4,128,128]{2,1,0:T(8,128)(2,1)S(1)} %get-tuple-element.39), channel_id=1, source_target_pairs={{0,2},{1,3},{2,0},{3,1},{4,6},{5,7},{6,4},{7,5},{8,10},{9,11},{10,... | collective-permute-start | bytes 393224 | tf_op jit(solution)/shard_map/ppermute | solution.py:252
  32.3 0.1 collective-permute-start.8
  32.4 0.3 shard_map.53
  32.7 0.0 copy-start.2
  32.7 2.1 %collective-permute-done.6.refs_1_ = bf16[4,128,128]{2,1,0:T(8,128)(2,1)S(1)} collective-permute-done((bf16[4,128,128]{2,1,0:T(8,128)(2,1)S(1)}, bf16[4,128,128]{2,1,0:T(8,128)(2,1)S(1)}, u32[]{:S(2)}, u32[]{:S(2)}) %collective-permute-start.6) | collective-permute-done | bytes 131104 | tf_op jit(solution)/shard_map/ppermute | solution.py:252
  34.7 2.2 %collective-permute-done.7.refs_2_ = bf16[4,128,128]{2,1,0:T(8,128)(2,1)S(1)} collective-permute-done((bf16[4,128,128]{2,1,0:T(8,128)(2,1)S(1)}, bf16[4,128,128]{2,1,0:T(8,128)(2,1)S(1)}, u32[]{:S(2)}, u32[]{:S(2)}) %collective-permute-start.7) | collective-permute-done | bytes 131104 | tf_op jit(solution)/shard_map/ppermute | solution.py:252
  36.9 1.8 %collective-permute-done.8.refs_3_ = bf16[4,128,128]{2,1,0:T(8,128)(2,1)S(1)} collective-permute-done((bf16[4,128,128]{2,1,0:T(8,128)(2,1)S(1)}, bf16[4,128,128]{2,1,0:T(8,128)(2,1)S(1)}, u32[]{:S(2)}, u32[]{:S(2)}) %collective-permute-start.8) | collective-permute-done | bytes 131104 | tf_op jit(solution)/shard_map/ppermute | solution.py:252
  38.7 1.7 %shard_map.54.mine = bf16[4,128,128]{2,1,0:T(8,128)(2,1)S(1)} custom-call(bf16[512,1024]{1,0:T(8,128)(2,1)S(1)} %get-tuple-element.36.system, f32[512,128]{1,0:T(8,128)S(1)} %get-tuple-element.37.diag_sum, bf16[4,128,128]{2,1,0:T(8,128)(2,1)S(1)} %get-tuple-element.35.refs_4_.refs_0_, bf16[4,128,128]{2,1,0:T(8,128)(2,1)S(1)} %collective-permute-done.6.refs_1_, ...), custom_call_target="tpu_custom_call" | custom-call | flops 805306368 | bytes 2097152 | tf_op jit(solution)/shard_map/pallas_call | solution.py:312
  40.4 0.1 collective-permute-start.11
  40.5 1.4 %shard_map.46.order_only.sketched = bf16[768,256]{1,0:T(8,128)(2,1)S(1)} custom-call(bf16[4,6,24,128]{3,2,1,0:T(8,128)(2,1)S(1)} %broadcast_in_dim.2.mask, bf16[4,6,24,128,128]{4,3,2,1,0:T(8,128)(2,1)S(1)} %copy-done, bf16[3072,256]{1,0:T(8,128)(2,1)S(1)} %copy-done.2), custom_call_target="tpu_custom_call" | custom-call | flops 1207959552 | bytes 6291456 | tf_op jit(solution)/shard_map/pallas_call | solution.py:284
  41.9 1.5 %shard_map.47 = (bf16[768,512]{1,0:T(8,128)(2,1)S(1)}, bf16[768,512]{1,0:T(8,128)(2,1)S(1)}, bf16[768,512]{1,0:T(8,128)(2,1)S(1)}, bf16[768,512]{1,0:T(8,128)(2,1)S(1)}) custom-call(s32[4,4]{1,0:T(4,128)S(1)} %copy-done.4, s32[6,4,24]{2,1,0:T(4,128)S(1)} %bitcast.2, bf16[4,6,24,128,128]{4,3,2,1,0:T(8,128)(2,1)S(1)} %copy-done, ...), custom_call_target="tpu_custom_call" | custom-call | bytes 6291456 | tf_op jit(solution)/shard_map/pallas_call | solution.py:307
  43.4 1.7 %collective-permute-start.10 = (bf16[4,128,128]{2,1,0:T(8,128)(2,1)S(1)}, bf16[4,128,128]{2,1,0:T(8,128)(2,1)S(1)}, u32[]{:S(2)}, u32[]{:S(2)}) collective-permute-start(bf16[4,128,128]{2,1,0:T(8,128)(2,1)S(1)} %shard_map.54.mine), channel_id=1, source_target_pairs={{0,4},{1,5},{2,6},{3,7},{4,0},{5,1},{6,2},{7,3},{8,12},{9,13},{10,... | collective-permute-start | bytes 393224 | tf_op jit(solution)/shard_map/ppermute | solution.py:252
  45.1 1.4 %shard_map.56.sketched = bf16[768,256]{1,0:T(8,128)(2,1)S(1)} custom-call(bf16[4,6,24,128]{3,2,1,0:T(8,128)(2,1)S(1)} %broadcast_in_dim.2.mask, bf16[4,6,24,128,128]{4,3,2,1,0:T(8,128)(2,1)S(1)} %copy-done, bf16[3072,256]{1,0:T(8,128)(2,1)S(1)} %copy-done.2), custom_call_target="tpu_custom_call" | custom-call | flops 1207959552 | bytes 6291456 | tf_op jit(solution)/shard_map/pallas_call | solution.py:284
  46.5 1.8 %collective-permute-start.14 = (bf16[4,128,128]{2,1,0:T(8,128)(2,1)S(1)}, bf16[4,128,128]{2,1,0:T(8,128)(2,1)S(1)}, u32[]{:S(2)}, u32[]{:S(2)}) collective-permute-start(bf16[4,128,128]{2,1,0:T(8,128)(2,1)S(1)} %shard_map.54.mine), channel_id=1, source_target_pairs={{0,2},{1,3},{2,0},{3,1},{4,6},{5,7},{6,4},{7,5},{8,10},{9,11},{10,... | collective-permute-start | bytes 393224 | tf_op jit(solution)/shard_map/ppermute | solution.py:252
  48.3 1.1 %shard_map.57.refs_0_ = bf16[4,768,256]{2,1,0:T(8,128)(2,1)} custom-call(bf16[768,256]{1,0:T(8,128)(2,1)S(1)} %shard_map.56.sketched, bf16[768,512]{1,0:T(8,128)(2,1)S(1)} %get-tuple-element.42.side, bf16[4,128,128]{2,1,0:T(8,128)(2,1)S(1)} %shard_map.54.mine, bf16[4,128,128]{2,1,0:T(8,128)(2,1)S(1)} %collective-permute-done.11.theirs), custom_call_target="tpu_custom_call" | custom-call | flops 201326592 | bytes 2097152 | tf_op jit(solution)/shard_map/pallas_call | solution.py:327
  49.4 0.0 collective-permute-done.10.mine
  49.4 0.1 collective-permute-start.12
  49.5 2.7 %collective-permute-start.9 = (bf16[4,128,128]{2,1,0:T(8,128)(2,1)S(1)}, bf16[4,128,128]{2,1,0:T(8,128)(2,1)S(1)}, u32[]{:S(2)}, u32[]{:S(2)}) collective-permute-start(bf16[4,128,128]{2,1,0:T(8,128)(2,1)S(1)} %shard_map.54.mine), channel_id=1, source_target_pairs={{0,6},{1,7},{2,4},{3,5},{4,2},{5,3},{6,0},{7,1},{8,14},{9,15},{10,... | collective-permute-start | bytes 393224 | tf_op jit(solution)/shard_map/ppermute | solution.py:252
  52.2 1.4 %shard_map.55.sketched = bf16[768,256]{1,0:T(8,128)(2,1)S(1)} custom-call(bf16[4,6,24,128]{3,2,1,0:T(8,128)(2,1)S(1)} %broadcast_in_dim.2.mask, bf16[4,6,24,128,128]{4,3,2,1,0:T(8,128)(2,1)S(1)} %copy-done, bf16[3072,256]{1,0:T(8,128)(2,1)S(1)} %copy-done.2), custom_call_target="tpu_custom_call" | custom-call | flops 1207959552 | bytes 6291456 | tf_op jit(solution)/shard_map/pallas_call | solution.py:284
  53.6 0.3 collective-permute-start.15
  53.9 0.0 collective-permute-done.12.theirs
  53.9 1.1 %shard_map.58.refs_0_ = bf16[4,768,256]{2,1,0:T(8,128)(2,1)} custom-call(bf16[768,256]{1,0:T(8,128)(2,1)S(1)} %shard_map.55.sketched, bf16[768,512]{1,0:T(8,128)(2,1)S(1)} %get-tuple-element.41.side, bf16[4,128,128]{2,1,0:T(8,128)(2,1)S(1)} %collective-permute-done.10.mine, ...), custom_call_target="tpu_custom_call", output_to_operand_aliasing={{}: (4, {})} | custom-call | flops 201326592 | bytes 2097152 | tf_op jit(solution)/shard_map/pallas_call | solution.py:327
  55.0 1.3 %collective-permute-done.9.mine = bf16[4,128,128]{2,1,0:T(8,128)(2,1)S(1)} collective-permute-done((bf16[4,128,128]{2,1,0:T(8,128)(2,1)S(1)}, bf16[4,128,128]{2,1,0:T(8,128)(2,1)S(1)}, u32[]{:S(2)}, u32[]{:S(2)}) %collective-permute-start.9) | collective-permute-done | bytes 131104 | tf_op jit(solution)/shard_map/ppermute | solution.py:252
  56.3 0.0 collective-permute-start.13
  56.3 1.4 %shard_map.59.sketched = bf16[768,256]{1,0:T(8,128)(2,1)S(1)} custom-call(bf16[4,6,24,128]{3,2,1,0:T(8,128)(2,1)S(1)} %broadcast_in_dim.2.mask, bf16[4,6,24,128,128]{4,3,2,1,0:T(8,128)(2,1)S(1)} %copy-done, bf16[3072,256]{1,0:T(8,128)(2,1)S(1)} %copy-done.2), custom_call_target="tpu_custom_call" | custom-call | flops 1207959552 | bytes 6291456 | tf_op jit(solution)/shard_map/pallas_call | solution.py:284
  57.7 1.1 %shard_map.60.refs_0_ = bf16[4,768,256]{2,1,0:T(8,128)(2,1)} custom-call(bf16[768,256]{1,0:T(8,128)(2,1)S(1)} %shard_map.59.sketched, bf16[768,512]{1,0:T(8,128)(2,1)S(1)} %get-tuple-element.46.side, bf16[4,128,128]{2,1,0:T(8,128)(2,1)S(1)} %collective-permute-done.14.mine, ...), custom_call_target="tpu_custom_call", output_to_operand_aliasing={{}: (4, {})} | custom-call | flops 201326592 | bytes 2097152 | tf_op jit(solution)/shard_map/pallas_call | solution.py:327
  58.9 1.1 %shard_map.61 = bf16[4,768,256]{2,1,0:T(8,128)(2,1)} custom-call(bf16[768,256]{1,0:T(8,128)(2,1)S(1)} %shard_map.46.order_only.sketched, bf16[768,512]{1,0:T(8,128)(2,1)S(1)} %get-tuple-element.26.side, bf16[4,128,128]{2,1,0:T(8,128)(2,1)S(1)} %collective-permute-done.9.mine, ...), custom_call_target="tpu_custom_call", output_to_operand_aliasing={{}: (4, {})} | custom-call | flops 201326592 | bytes 2097152 | tf_op jit(solution)/shard_map/pallas_call | solution.py:327
  (14 shorter events, 0.0 us)
Async XLA Ops:
  0.0 3.4 %copy-start.4 = (s32[4,4]{1,0:T(4,128)S(1)}, s32[4,4]{1,0:T(4,128)}, u32[]{:S(2)}) copy-start(s32[4,4]{1,0:T(4,128)} %shared.5) | copy-start | bytes 196
  0.0 3.5 %copy-start.3 = (s32[4,6,24]{2,0,1:T(4,128)S(1)}, s32[4,6,24]{2,0,1:T(4,128)}, u32[]{:S(2)}) copy-start(s32[4,6,24]{2,0,1:T(4,128)} %param.5) | copy-start | bytes 6916
  0.0 6.6 %copy-start = (bf16[4,6,24,128,128]{4,3,2,1,0:T(8,128)(2,1)S(1)}, bf16[4,6,24,128,128]{4,3,2,1,0:T(8,128)(2,1)}, u32[]{:S(2)}) copy-start(bf16[4,6,24,128,128]{4,3,2,1,0:T(8,128)(2,1)} %blocks.13) | copy-start | bytes 56623108
  3.0 7.8 %collective-permute-start = (bf16[4,2,128,512]{3,2,1,0:T(8,128)(2,1)S(1)}, bf16[4,2,128,512]{3,2,1,0:T(8,128)(2,1)S(1)}, u32[]{:S(2)}, u32[]{:S(2)}) collective-permute-start(bf16[4,2,128,512]{3,2,1,0:T(8,128)(2,1)S(1)} %get-tuple-element.28), channel_id=1, source_target_pairs={{0,1},{1,0},{2,3},{3,2},{4,5},{5,4},{6,7},{7,6},{8,9},{9,8},{10,11... | collective-permute-start | bytes 3145736 | tf_op jit(solution)/shard_map/ppermute | solution.py:244
  6.6 1.4 %copy-start.1 = (bf16[3072,256]{1,0:T(8,128)(2,1)S(1)}, bf16[3072,256]{1,0:T(8,128)(2,1)}, u32[]{:S(2)}) copy-start(bf16[3072,256]{1,0:T(8,128)(2,1)} %sketch.9) | copy-start | bytes 4718596
  10.6 6.0 %collective-permute-start.4 = (bf16[4,4,128,128]{3,2,1,0:T(8,128)(2,1)S(1)}, bf16[4,4,128,128]{3,2,1,0:T(8,128)(2,1)S(1)}, u32[]{:S(2)}, u32[]{:S(2)}) collective-permute-start(bf16[4,4,128,128]{3,2,1,0:T(8,128)(2,1)S(1)} %get-tuple-element.34), channel_id=1, source_target_pairs={{0,1},{1,0},{2,3},{3,2},{4,5},{5,4},{6,7},{7,6},{8,9},{9,8},{10,11... | collective-permute-start | bytes 1572872 | tf_op jit(solution)/shard_map/ppermute | solution.py:244
  10.9 9.5 %collective-permute-start.1 = (bf16[2,128,512]{2,1,0:T(8,128)(2,1)S(1)}, bf16[2,128,512]{2,1,0:T(8,128)(2,1)S(1)}, u32[]{:S(2)}, u32[]{:S(2)}) collective-permute-start(bf16[2,128,512]{2,1,0:T(8,128)(2,1)S(1)} %get-tuple-element.30), channel_id=1, source_target_pairs={{0,4},{1,5},{2,6},{3,7},{4,0},{5,1},{6,2},{7,3},{8,12},{9,13},{10,... | collective-permute-start | bytes 786440 | tf_op jit(solution)/shard_map/ppermute | solution.py:252
  13.5 10.3 %collective-permute-start.2 = (bf16[2,128,512]{2,1,0:T(8,128)(2,1)S(1)}, bf16[2,128,512]{2,1,0:T(8,128)(2,1)S(1)}, u32[]{:S(2)}, u32[]{:S(2)}) collective-permute-start(bf16[2,128,512]{2,1,0:T(8,128)(2,1)S(1)} %get-tuple-element.31), channel_id=1, source_target_pairs={{0,2},{1,3},{2,0},{3,1},{4,6},{5,7},{6,4},{7,5},{8,10},{9,11},{10,... | collective-permute-start | bytes 786440 | tf_op jit(solution)/shard_map/ppermute | solution.py:252
  16.6 12.1 %collective-permute-start.3 = (bf16[2,128,512]{2,1,0:T(8,128)(2,1)S(1)}, bf16[2,128,512]{2,1,0:T(8,128)(2,1)S(1)}, u32[]{:S(2)}, u32[]{:S(2)}) collective-permute-start(bf16[2,128,512]{2,1,0:T(8,128)(2,1)S(1)} %get-tuple-element.32), channel_id=1, source_target_pairs={{0,6},{1,7},{2,4},{3,5},{4,2},{5,3},{6,0},{7,1},{8,14},{9,15},{10,... | collective-permute-start | bytes 786440 | tf_op jit(solution)/shard_map/ppermute | solution.py:252
  28.8 3.6 %collective-permute-start.5 = (bf16[2,2,128,512]{3,2,1,0:T(8,128)(2,1)S(1)}, bf16[2,2,128,512]{3,2,1,0:T(8,128)(2,1)S(1)}, u32[]{:S(2)}, u32[]{:S(2)}) collective-permute-start(bf16[2,2,128,512]{3,2,1,0:T(8,128)(2,1)S(1)} %shard_map.52.mine), channel_id=1, source_target_pairs={{0,1},{1,0},{2,3},{3,2},{4,5},{5,4},{6,7},{7,6},{8,9},{9,8},{10,11... | collective-permute-start | bytes 1572872 | tf_op jit(solution)/shard_map/ppermute | solution.py:244
  28.8 5.9 %collective-permute-start.6 = (bf16[4,128,128]{2,1,0:T(8,128)(2,1)S(1)}, bf16[4,128,128]{2,1,0:T(8,128)(2,1)S(1)}, u32[]{:S(2)}, u32[]{:S(2)}) collective-permute-start(bf16[4,128,128]{2,1,0:T(8,128)(2,1)S(1)} %get-tuple-element.38), channel_id=1, source_target_pairs={{0,4},{1,5},{2,6},{3,7},{4,0},{5,1},{6,2},{7,3},{8,12},{9,13},{10,... | collective-permute-start | bytes 393224 | tf_op jit(solution)/shard_map/ppermute | solution.py:252
  30.6 6.4 %collective-permute-start.7 = (bf16[4,128,128]{2,1,0:T(8,128)(2,1)S(1)}, bf16[4,128,128]{2,1,0:T(8,128)(2,1)S(1)}, u32[]{:S(2)}, u32[]{:S(2)}) collective-permute-start(bf16[4,128,128]{2,1,0:T(8,128)(2,1)S(1)} %get-tuple-element.39), channel_id=1, source_target_pairs={{0,2},{1,3},{2,0},{3,1},{4,6},{5,7},{6,4},{7,5},{8,10},{9,11},{10,... | collective-permute-start | bytes 393224 | tf_op jit(solution)/shard_map/ppermute | solution.py:252
  32.3 6.4 %collective-permute-start.8 = (bf16[4,128,128]{2,1,0:T(8,128)(2,1)S(1)}, bf16[4,128,128]{2,1,0:T(8,128)(2,1)S(1)}, u32[]{:S(2)}, u32[]{:S(2)}) collective-permute-start(bf16[4,128,128]{2,1,0:T(8,128)(2,1)S(1)} %get-tuple-element.40), channel_id=1, source_target_pairs={{0,6},{1,7},{2,4},{3,5},{4,2},{5,3},{6,0},{7,1},{8,14},{9,15},{10,... | collective-permute-start | bytes 393224 | tf_op jit(solution)/shard_map/ppermute | solution.py:252
  32.7 7.8 %copy-start.2 = (bf16[3072,256]{1,0:T(8,128)(2,1)S(1)}, bf16[3072,256]{1,0:T(8,128)(2,1)}, u32[]{:S(2)}) copy-start(bf16[3072,256]{1,0:T(8,128)(2,1)} %sketch.9) | copy-start | bytes 4718596
  40.4 7.9 %collective-permute-start.11 = (bf16[4,128,128]{2,1,0:T(8,128)(2,1)S(1)}, bf16[4,128,128]{2,1,0:T(8,128)(2,1)S(1)}, u32[]{:S(2)}, u32[]{:S(2)}) collective-permute-start(bf16[4,128,128]{2,1,0:T(8,128)(2,1)S(1)} %shard_map.54.mine), channel_id=1, source_target_pairs={{0,1},{1,0},{2,3},{3,2},{4,5},{5,4},{6,7},{7,6},{8,9},{9,8},{10,11... | collective-permute-start | bytes 393224 | tf_op jit(solution)/shard_map/ppermute | solution.py:244
  43.4 6.1 %collective-permute-start.10 = (bf16[4,128,128]{2,1,0:T(8,128)(2,1)S(1)}, bf16[4,128,128]{2,1,0:T(8,128)(2,1)S(1)}, u32[]{:S(2)}, u32[]{:S(2)}) collective-permute-start(bf16[4,128,128]{2,1,0:T(8,128)(2,1)S(1)} %shard_map.54.mine), channel_id=1, source_target_pairs={{0,4},{1,5},{2,6},{3,7},{4,0},{5,1},{6,2},{7,3},{8,12},{9,13},{10,... | collective-permute-start | bytes 393224 | tf_op jit(solution)/shard_map/ppermute | solution.py:252
  46.5 7.1 %collective-permute-start.14 = (bf16[4,128,128]{2,1,0:T(8,128)(2,1)S(1)}, bf16[4,128,128]{2,1,0:T(8,128)(2,1)S(1)}, u32[]{:S(2)}, u32[]{:S(2)}) collective-permute-start(bf16[4,128,128]{2,1,0:T(8,128)(2,1)S(1)} %shard_map.54.mine), channel_id=1, source_target_pairs={{0,2},{1,3},{2,0},{3,1},{4,6},{5,7},{6,4},{7,5},{8,10},{9,11},{10,... | collective-permute-start | bytes 393224 | tf_op jit(solution)/shard_map/ppermute | solution.py:252
  49.4 4.4 %collective-permute-start.12 = (bf16[4,128,128]{2,1,0:T(8,128)(2,1)S(1)}, bf16[4,128,128]{2,1,0:T(8,128)(2,1)S(1)}, u32[]{:S(2)}, u32[]{:S(2)}) collective-permute-start(bf16[4,128,128]{2,1,0:T(8,128)(2,1)S(1)} %collective-permute-done.10.mine), channel_id=1, source_target_pairs={{0,1},{1,0},{2,3},{3,2},{4,5},{5,4},{6,7},{7,6},{8,9},{9,8},{10,11... | collective-permute-start | bytes 393224 | tf_op jit(solution)/shard_map/ppermute | solution.py:244
  49.5 6.8 %collective-permute-start.9 = (bf16[4,128,128]{2,1,0:T(8,128)(2,1)S(1)}, bf16[4,128,128]{2,1,0:T(8,128)(2,1)S(1)}, u32[]{:S(2)}, u32[]{:S(2)}) collective-permute-start(bf16[4,128,128]{2,1,0:T(8,128)(2,1)S(1)} %shard_map.54.mine), channel_id=1, source_target_pairs={{0,6},{1,7},{2,4},{3,5},{4,2},{5,3},{6,0},{7,1},{8,14},{9,15},{10,... | collective-permute-start | bytes 393224 | tf_op jit(solution)/shard_map/ppermute | solution.py:252
  53.6 4.2 %collective-permute-start.15 = (bf16[4,128,128]{2,1,0:T(8,128)(2,1)S(1)}, bf16[4,128,128]{2,1,0:T(8,128)(2,1)S(1)}, u32[]{:S(2)}, u32[]{:S(2)}) collective-permute-start(bf16[4,128,128]{2,1,0:T(8,128)(2,1)S(1)} %collective-permute-done.14.mine), channel_id=1, source_target_pairs={{0,1},{1,0},{2,3},{3,2},{4,5},{5,4},{6,7},{7,6},{8,9},{9,8},{10,11... | collective-permute-start | bytes 393224 | tf_op jit(solution)/shard_map/ppermute | solution.py:244
  56.3 2.5 %collective-permute-start.13 = (bf16[4,128,128]{2,1,0:T(8,128)(2,1)S(1)}, bf16[4,128,128]{2,1,0:T(8,128)(2,1)S(1)}, u32[]{:S(2)}, u32[]{:S(2)}) collective-permute-start(bf16[4,128,128]{2,1,0:T(8,128)(2,1)S(1)} %collective-permute-done.9.mine), channel_id=1, source_target_pairs={{0,1},{1,0},{2,3},{3,2},{4,5},{5,4},{6,7},{7,6},{8,9},{9,8},{10,11... | collective-permute-start | bytes 393224 | tf_op jit(solution)/shard_map/ppermute | solution.py:244
where the time goes:
time: 60.2 us; the launch traced here: 60 us
  waiting for transfers between devices  19.4 us (32%)
  Pallas kernels  19.2 us (32%)
  starting transfers between devices  16.6 us (28%)
  local copies, waits for them, and re-layouts  4.52 us (8%)
    ppermute x9, waiting for transfers between devices, chip_at(): return lax.ppermute(value, ('box', 'face'), pairs)  19.4 us
    ppermute x9, starting transfers between devices, chip_at(): return lax.ppermute(value, ('box', 'face'), pairs)  15.5 us
    pallas_call x4, Pallas kernels, local(): call(functools.partial(sketch_kernel, distance), jax.ShapeDtypeStruct((or...  5.56 us
    pallas_call x4, Pallas kernels, local(): call(functools.partial(correct_kernel, distance), out_shape, 4, [VMEM] *...  4.45 us
    unnamed x10, local copies, waits for them, and re-layouts  4.38 us
    pallas_call x1, Pallas kernels, local(): call(gather_kernel, [part_shape] * 2, 4, [SMEM, HBM, HBM], [VMEM, VMEM],...  2.94 us
    pallas_call x1, Pallas kernels, local(): call(right_kernel, [half_shape] * 2, 6, [SMEM] + [VMEM] * 3, [VMEM] * 2,...  2.58 us
    pallas_call x1, Pallas kernels, local(): call(solve_kernel, jax.ShapeDtypeStruct((slots, blk, cols // 2), kind), 8...  1.67 us
  transfers between devices with their start and end apart: 16, of which 7 were waited for; matrix products, arithmetic and copies ran while one was open for 0% of the time, Pallas kernels for 22%

commit v1 on v0

v1 whole, which is shorter than its diff:
```python
import functools

import jax
import jax.numpy as jnp
from jax import lax
from jax.experimental import pallas as pl
from jax.experimental.pallas import tpu as pltpu
from jax.sharding import PartitionSpec as P


ITERS = 4
MIB = 1024 * 1024
SMEM = pl.BlockSpec(memory_space=pltpu.SMEM)
VMEM = pl.BlockSpec(memory_space=pltpu.VMEM)
ANY = pl.BlockSpec(memory_space=pl.ANY)
HBM = pl.BlockSpec(memory_space=pltpu.HBM)


def call(kernel, out_shape, mib, in_specs, out_specs, flops=0, moved=0, **kwargs):
    return pl.pallas_call(
        kernel,
        out_shape=out_shape,
        in_specs=in_specs,
        out_specs=out_specs,
        compiler_params=pltpu.CompilerParams(vmem_limit_bytes=mib * MIB),
        cost_estimate=pl.CostEstimate(flops=flops, bytes_accessed=moved, transcendentals=0),
        **kwargs,
    )


def place():
    face, box = lax.axis_index("face"), lax.axis_index("box")
    return lax.rem(face, 2), lax.bitwise_or(lax.shift_left(lax.div(face, 2), 1), lax.rem(box, 2))


def swapped(step):
    return (step & ~3) | ((step & 1) << 1) | ((step >> 1) & 1)


def distance_of(step):
    return jnp.where(place()[0] == 0, step, swapped(step))


def box_at(step, boxes):
    return lax.rem(lax.bitwise_xor(place()[1], distance_of(step)), boxes)


def gather_kernel(groups, shared, pattern_hbm, blocks, *refs):
    outs, (pattern, sems) = refs[:-2], refs[-2:]
    _, half, blk, width = outs[0].shape
    boxes, row_count = blocks.shape[:2]
    slots = 2 * half
    row_start = lax.axis_index("face") * row_count
    core, chip = place()

    def each(action):
        copied = 0
        for order, group in enumerate(groups):
            for where, target in ((1 - core, outs[2 * order]), (core, outs[2 * order + 1])):
                for index, distance in enumerate(group):
                    box = lax.rem(lax.bitwise_xor(chip, distance), boxes)
                    for part in range(half):
                        slot = where * half + part
                        row = shared[box, slot] - row_start
                        owned = jnp.logical_and(row >= 0, row < row_count)
                        action(box, row, owned, target.at[index, part], sems.at[copied])
                        copied += 1

    def start(box, row, owned, target, sem):
        @pl.when(owned)
        def _():
            for other in range(slots):
                pltpu.make_async_copy(
                    blocks.at[box, row, shared[box, other]], target.at[:, pl.ds(other * blk, blk)], sem
                ).start()

    def clear(box, row, owned, target, sem):
        @pl.when(jnp.logical_not(owned))
        def _():
            target[...] = jnp.zeros((blk, width), target.dtype)

    def finish(box, row, owned, target, sem):
        @pl.when(owned)
        def _():
            pltpu.make_async_copy(target, target, sem).wait()
            for other in range(slots):

                @pl.when(pattern[row, box, shared[box, other]] == 0)
                def _():
                    target[:, pl.ds(other * blk, blk)] = jnp.zeros((blk, blk), target.dtype)

    to_scalars = pltpu.make_async_copy(pattern_hbm, pattern, sems.at[boxes * slots])
    to_scalars.start()
    each(start)
    each(clear)
    to_scalars.wait()
    each(finish)


def merge_kernel(steps, index_of, keep, received, *outs):
    for step, out in zip(steps, outs):
        index = index_of(step)
        out[...] = keep[index] + received[index]


def side_sum_kernel(*refs):
    ins, out = refs[:-2], refs[-1]
    first = place()[0] == 0
    totals = [None, None]

    def add(side, value):
        totals[side] = value if totals[side] is None else totals[side] + value

    for step, ref in enumerate(ins):
        other = swapped(step)
        if other == step:
            add(step & 1, ref[...])
        elif step & 1:
            add(1, jnp.where(first, ref[...], ins[other][...]))
            add(0, jnp.where(first, ins[other][...], ref[...]))
    for side, total in enumerate(totals):
        out[side] = total


def system_kernel(mine, theirs, system, rough, diag_sum):
    _, half, blk, width = mine.shape
    slots = 2 * half
    core = place()[0]
    for part, where in ((mine, core), (theirs, 1 - core)):
        for side in range(2):
            rows = pl.ds(pl.multiple_of(where * half * blk, half * blk), half * blk)
            system[rows, side * width : (side + 1) * width] = part[side].reshape(half * blk, width)
        total = part[0].astype(jnp.float32) + part[1].astype(jnp.float32)
        rough[rows, :] = total.reshape(half * blk, width).astype(rough.dtype)
    eye = lax.broadcasted_iota(jnp.int32, (blk, blk), 0) == lax.broadcasted_iota(jnp.int32, (blk, blk), 1)
    for slot in range(slots):
        rows = slice(slot * blk, (slot + 1) * blk)
        both = system[rows, rows].astype(jnp.float32) + system[
            rows, width + slot * blk : width + (slot + 1) * blk
        ].astype(jnp.float32)
        line = jnp.sum(jnp.where(eye, both, 0.0), axis=1, keepdims=True)
        diag_sum[rows, :] = jnp.broadcast_to(line, (blk, diag_sum.shape[1]))
        rough[rows, rows] = jnp.where(eye, 0.0, both).astype(rough.dtype)


def masked_row(mask, blocks, box, row):
    parts = [
        blocks[box, row, column] * mask[box, row, column : column + 1] for column in range(blocks.shape[2])
    ]
    return jnp.concatenate(parts, axis=1)


def right_kernel(shared, mask, blocks, sketch, send, keep):
    boxes, row_count = blocks.shape[:2]
    slots, half_cols = keep.shape[1], keep.shape[3]
    row_start = lax.axis_index("face") * row_count
    core = place()[0]

    def one(step, carry):
        box, slot = step // slots, lax.rem(step, slots)
        row = shared[box, slot] - row_start
        owned = jnp.logical_and(row >= 0, row < row_count)

        @pl.when(owned)
        def _():
            left = masked_row(mask, blocks, box, row)
            product = jnp.dot(left, sketch[...], preferred_element_type=jnp.float32).astype(keep.dtype)
            low, high = product[:, :half_cols], product[:, half_cols:]
            keep[box, slot] = jnp.where(core == 0, low, high)
            send[box, slot] = jnp.where(core == 0, high, low)

        @pl.when(jnp.logical_not(owned))
        def _():
            keep[box, slot] = jnp.zeros(keep.shape[2:], keep.dtype)
            send[box, slot] = jnp.zeros(send.shape[2:], send.dtype)

        return carry

    lax.fori_loop(0, boxes * slots, one, 0)


def sketch_kernel(step, mask, blocks, sketch, *refs):
    sketched = refs[-1]
    boxes, row_count, _, blk, _ = blocks.shape
    box = box_at(step, boxes)
    for row in range(row_count):
        left = masked_row(mask, blocks, box, row)
        product = jnp.dot(left, sketch[...], preferred_element_type=jnp.float32)
        sketched[row * blk : (row + 1) * blk] = product.astype(sketched.dtype)


def side_kernel(shared, pattern, blocks, order_only, *sides):
    del order_only
    boxes, row_count, _, blk, _ = blocks.shape
    for step, side in enumerate(sides):
        box = box_at(step, boxes)
        for slot in range(shared.shape[1]):
            column = shared[box, slot]
            for row in range(row_count):
                stored = jnp.where(pattern[row, box, column] != 0, 1.0, 0.0).astype(blocks.dtype)
                side[row * blk : (row + 1) * blk, slot * blk : (slot + 1) * blk] = (
                    blocks[box, row, column] * stored
                )


def solve_kernel(system, rough, diag_sum, *refs):
    rhs_refs, out = refs[:-1], refs[-1]
    right_side = rhs_refs[0][...].astype(jnp.float32)
    for ref in rhs_refs[1:]:
        right_side = right_side + ref[...].astype(jnp.float32)
    slots, blk, cols = right_side.shape
    right_side = right_side.reshape(slots * blk, cols)
    potential = right_side / diag_sum[...]
    for sweep in range(ITERS - 1):
        high = potential.astype(jnp.bfloat16)
        low = (potential - high.astype(jnp.float32)).astype(jnp.bfloat16)
        both = jnp.concatenate([high, low], axis=1)
        if sweep < ITERS - 2:
            applied = jnp.dot(rough[...], both, preferred_element_type=jnp.float32)
            potential = (right_side - applied[:, :cols] - applied[:, cols:]) / diag_sum[...]
        else:
            stacked = jnp.concatenate([both, both], axis=0)
            applied = jnp.dot(system[...], stacked, preferred_element_type=jnp.float32)
            applied = applied[:, :cols] + applied[:, cols:]
            potential = potential + (right_side - applied) / diag_sum[...]
    out[...] = potential.astype(out.dtype).reshape(out.shape)


def correct_kernel(steps, *refs):
    out, result, sems = refs[-3:]
    boxes = out.shape[0]
    core = place()[0]
    copies = []
    for index, step in enumerate(steps):
        sketched, side, mine, theirs = refs[4 * index : 4 * index + 4]
        slots, blk, cols = mine.shape
        own = mine[...].reshape(slots * blk, cols)
        other = theirs[...].reshape(slots * blk, cols)
        parts = [jnp.where(core == 0, own, other), jnp.where(core == 0, other, own)]
        potential = jnp.concatenate(parts, axis=1)
        correction = jnp.dot(side[...], potential, preferred_element_type=jnp.float32)
        result[index] = (sketched[...].astype(jnp.float32) - correction).astype(result.dtype)
        copy = pltpu.make_async_copy(result.at[index], out.at[box_at(step, boxes)], sems.at[index])
        copy.start()
        copies.append(copy)
    for copy in copies:
        copy.wait()


def local(blocks, pattern, shared, sketch):
    boxes, row_count, all_blocks, blk, _ = blocks.shape
    slots = shared.shape[1]
    half = slots // 2
    cols = sketch.shape[1]
    box_size, face_size = lax.axis_size("box"), lax.axis_size("face")
    chips = face_size
    kind = blocks.dtype
    by_row = jnp.transpose(pattern, (1, 0, 2))
    outside = jnp.all(shared[:, :, None] != lax.iota(jnp.int32, all_blocks)[None, None, :], axis=1)
    mask = jnp.logical_and(pattern != 0, outside[:, None, :]).astype(kind)
    mask = jnp.broadcast_to(mask[..., None], (boxes, row_count, all_blocks, blk))

    def other_core(value):
        pairs = [(f, f ^ 1) for f in range(face_size)]
        return lax.ppermute(value, "face", pairs)

    def chip_at(value, step):
        pairs = []
        for b in range(box_size):
            for f in range(face_size):
                distance = swapped(step) if f & 1 else step
                target = (b ^ (distance & 1)) * face_size + (f ^ (2 * (distance >> 1)))
                pairs.append((b * face_size + f, target))
        return lax.ppermute(value, ("box", "face"), pairs)

    def around(values):
        arrived = {s: chip_at(values[s], s) for s in range(len(values) - 1, 0, -1)}
        return [values[0]] + [arrived[s] for s in range(1, len(values))]

    def merged(keep, received, steps, index_of):
        shape = jax.ShapeDtypeStruct(keep.shape[1:], kind)
        return call(
            functools.partial(merge_kernel, steps, index_of), [shape] * len(steps), 6,
            [VMEM, VMEM], [VMEM] * len(steps), moved=4 * keep.size * 2,
        )(keep, received)

    early, late = [boxes - 1], list(range(boxes - 1))
    part_shapes = [
        jax.ShapeDtypeStruct((len(group), half, blk, slots * blk), kind)
        for group in (early, late)
        for _ in range(2)
    ]
    in_place = lambda value: pltpu.with_memory_space_constraint(value, pltpu.HBM)
    send_early, keep_early, send_late, keep_late = call(
        functools.partial(gather_kernel, (early, late)), part_shapes, 4,
        [SMEM, HBM, HBM], [VMEM] * 4, moved=2 * MIB,
        scratch_shapes=[
            pltpu.SMEM(by_row.shape, jnp.int32),
            pltpu.SemaphoreType.DMA((boxes * slots + 1,)),
        ],
    )(in_place(shared), in_place(by_row), in_place(blocks))
    first_steps = [s for s in range(chips) if s % boxes in early]
    last_steps = [s for s in range(chips) if s % boxes in late]
    outs = dict(
        zip(
            first_steps,
            merged(
                keep_early, other_core(send_early), first_steps,
                lambda s: 0,
            ),
        )
    )
    outs.update(
        zip(
            last_steps,
            merged(
                keep_late, other_core(send_late), last_steps,
                lambda s: lax.rem(distance_of(s), boxes),
            ),
        )
    )
    arrived = around(outs)

    order = row_count * blk
    half_shape = jax.ShapeDtypeStruct((boxes, slots, blk, cols // 2), kind)
    send_y, keep_y = call(
        right_kernel, [half_shape] * 2, 6, [SMEM] + [VMEM] * 3, [VMEM] * 2,
        flops=2 * slots * blk * all_blocks * blk * cols, moved=4 * MIB,
    )(shared, mask, blocks, sketch)

    def sketch_at(step, *after):
        return call(
            functools.partial(sketch_kernel, step),
            jax.ShapeDtypeStruct((order, cols), kind), 6, [VMEM] * 3 + [ANY] * len(after), VMEM,
            flops=2 * order * all_blocks * blk * cols, moved=6 * MIB,
        )(mask, blocks, sketch, *after)

    outs_y = merged(
        keep_y, other_core(send_y), list(range(chips)),
        lambda s: box_at(s, boxes),
    )
    arrived_y = around(outs_y)

    both_shape = jax.ShapeDtypeStruct((2,) + outs[0].shape, kind)
    mine = call(
        side_sum_kernel, both_shape, 4, [VMEM] * chips + [ANY], VMEM, moved=3 * MIB // 2
    )(*arrived, outs_y[0])
    system, rough, diag_sum = call(
        system_kernel,
        [
            jax.ShapeDtypeStruct((slots * blk, 2 * slots * blk), kind),
            jax.ShapeDtypeStruct((slots * blk, slots * blk), kind),
            jax.ShapeDtypeStruct((slots * blk, cols // 2), jnp.float32),
        ],
        6, [VMEM] * 2, [VMEM] * 3, moved=2 * MIB,
    )(mine, other_core(mine))

    sketches = [sketch_at(s) for s in range(boxes - 1)] + [sketch_at(boxes - 1, diag_sum)]
    sides = call(
        side_kernel, [jax.ShapeDtypeStruct((order, slots * blk), kind)] * boxes, 6,
        [SMEM, SMEM, VMEM, ANY], [VMEM] * boxes, moved=6 * MIB,
    )(shared, by_row, blocks, sketches[-1])

    potential = call(
        solve_kernel,
        jax.ShapeDtypeStruct((slots, blk, cols // 2), kind), 8,
        [VMEM] * (3 + chips), VMEM,
        flops=2 * (ITERS - 1) * 2 * (slots * blk) ** 2 * cols, moved=2 * MIB,
    )(system, rough, diag_sum, *arrived_y)

    back = around([potential] * boxes)
    out_shape = jax.ShapeDtypeStruct((boxes, order, cols), kind)
    theirs = [None] * boxes
    result = []

    def correct(*steps):
        inputs = []
        for s in steps:
            inputs += [sketches[s], sides[s], back[s], theirs[swapped(s)]]
        count = len(inputs)
        corrected = call(
            functools.partial(correct_kernel, steps), out_shape, 2 + 2 * len(steps),
            [VMEM] * count + [HBM] * len(result), HBM,
            flops=2 * len(steps) * order * slots * blk * cols, moved=2 * len(steps) * MIB,
            scratch_shapes=[
                pltpu.VMEM((len(steps), order, cols), kind),
                pltpu.SemaphoreType.DMA((len(steps),)),
            ],
            input_output_aliases={count: 0} if result else {},
        )(*inputs, *result)
        result[:] = [corrected]

    def exchange(*steps):
        if result:
            values, result[0] = lax.optimization_barrier(([back[s] for s in steps], result[0]))
        else:
            values = [back[s] for s in steps]
        for s, value in zip(steps, values):
            theirs[s] = other_core(value)

    exchange(0)
    correct(0)
    exchange(boxes - 1)
    theirs[1:-1] = [other_core(back[s]) for s in range(1, boxes - 1)]
    correct(boxes - 1)
    correct(*range(1, boxes - 1))
    return result[0]


def solution(mesh):
    return jax.shard_map(
        local,
        mesh=mesh,
        in_specs=(P("box", "face", None, None, None), P("box", "face", None), P("box", None), P()),
        out_specs=P("box", "face", None),
        check_vma=False,
    )
```

time: 60.2 us -> 54.9 us (0.912)
  waiting for transfers between devices: 19.4 us -> 17.1 us
  starting transfers between devices: 16.6 us -> 14.5 us
  Pallas kernels: 19.2 us -> 18 us
    ppermute x9, starting transfers between devices: 15.5 us -> 12.9 us  [chip_at(): return lax.ppermute(value, ('box', 'face'), pairs)]
    ppermute x9, waiting for transfers between devices: 19.4 us -> 17.1 us  [chip_at(): return lax.ppermute(value, ('box', 'face'), pairs)]
    pallas_call x11, Pallas kernels: 13.2 us -> 12.2 us  [the longest x4 5.57 us: sketch_at(): call(functools.partial(sketch_kernel, step), jax.ShapeDtypeStruct((order,...]
    ppermute x7 -> x8, starting transfers between devices: 1.1 us -> 1.58 us  [other_core(): return lax.ppermute(value, 'face', pairs)]
  transfers between devices with their start and end apart: 16 -> 17, of which waited for: 7 -> 5; matrix products, arithmetic and copies ran while one was open for 0% -> 0% of each run, Pallas kernels for 22% -> 23%
where the time goes in v1:
time: 54.9 us; the launch traced here: 54.7 us
  Pallas kernels  18 us (33%)
  waiting for transfers between devices  17.1 us (31%)
  starting transfers between devices  14.5 us (26%)
  local copies, waits for them, and re-layouts  4.71 us (9%)
    ppermute x9, waiting for transfers between devices, chip_at(): return lax.ppermute(value, ('box', 'face'), pairs)  17.1 us
    ppermute x9, starting transfers between devices, chip_at(): return lax.ppermute(value, ('box', 'face'), pairs)  12.9 us
    pallas_call x4, Pallas kernels, sketch_at(): call(functools.partial(sketch_kernel, step), jax.ShapeDtypeStruct((order,...  5.57 us
    unnamed x10, local copies, waits for them, and re-layouts  4.57 us
    pallas_call x3, Pallas kernels, correct(): call(functools.partial(correct_kernel, steps), out_shape, 2 + 2 * len(ste...  3.76 us
    pallas_call x1, Pallas kernels, local(): call(functools.partial(gather_kernel, (early, late)), part_shapes, 4, [SM...  2.63 us
    pallas_call x1, Pallas kernels, local(): call(right_kernel, [half_shape] * 2, 6, [SMEM] + [VMEM] * 3, [VMEM] * 2,...  2.58 us
    ppermute x8, starting transfers between devices, other_core(): return lax.ppermute(value, 'face', pairs)  1.58 us
  transfers between devices with their start and end apart: 17, of which 5 were waited for; matrix products, arithmetic and copies ran while one was open for 0% of the time, Pallas kernels for 23%

profile of v1, /device:TPU:0, one launch (start us, length us, event | category | flops | bytes accessed | tf_op | source)
XLA Modules:
  0.0 54.7 jit_solution(17597846514087822197)
XLA Ops:
  0.0 2.6 %shard_map.47 = (bf16[1,2,128,512]{3,2,1,0:T(8,128)(2,1)S(1)}, bf16[1,2,128,512]{3,2,1,0:T(8,128)(2,1)S(1)}, bf16[3,2,128,512]{3,2,1,0:T(8,128)(2,1)S(1)}, bf16[3,2,128,512]{3,2,1,0:T(8,128)(2,1)S(1)}) custom-call(s32[4,4]{1,0:T(4,128)} %shared.5, s32[6,4,24]{2,1,0:T(4,128)} %bitcast.1, bf16[4,6,24,128,128]{4,3,2,1,0:T(8,128)(2,1)} %blocks.13), custom_call_target="tpu_custom_call" | custom-call | bytes 2097152 | tf_op jit(solution)/shard_map/pallas_call | solution.py:294
  2.6 0.3 collective-permute-start
  2.9 0.3 collective-permute-start.3
  3.2 0.1 fusion
  3.4 0.1 broadcast_in_dim.2.mask
  3.5 3.2 %copy-done = bf16[4,6,24,128,128]{4,3,2,1,0:T(8,128)(2,1)S(1)} copy-done((bf16[4,6,24,128,128]{4,3,2,1,0:T(8,128)(2,1)S(1)}, bf16[4,6,24,128,128]{4,3,2,1,0:T(8,128)(2,1)}, u32[]{:S(2)}) %copy-start) | copy-done | bytes 18874392
  6.7 1.4 %copy-done.1 = bf16[3072,256]{1,0:T(8,128)(2,1)S(1)} copy-done((bf16[3072,256]{1,0:T(8,128)(2,1)S(1)}, bf16[3072,256]{1,0:T(8,128)(2,1)}, u32[]{:S(2)}) %copy-start.1) | copy-done | bytes 1572888
  8.1 2.6 %shard_map.50 = (bf16[4,4,128,128]{3,2,1,0:T(8,128)(2,1)S(1)}, bf16[4,4,128,128]{3,2,1,0:T(8,128)(2,1)S(1)}) custom-call(s32[4,4]{1,0:T(4,128)S(1)} %copy-done.4, bf16[4,6,24,128]{3,2,1,0:T(8,128)(2,1)S(1)} %broadcast_in_dim.2.mask, bf16[4,6,24,128,128]{4,3,2,1,0:T(8,128)(2,1)S(1)} %copy-done, bf16[3072,256]{1,0:T(8,128)(2,1)S(1)} %copy-done.1), custom_call_target="tpu_custom_call" | custom-call | flops 805306368 | bytes 4194304 | tf_op jit(solution)/shard_map/pallas_call | solution.py:326
  10.6 0.1 collective-permute-start.5
  10.8 0.0 collective-permute-done.3.received
  10.8 5.2 %collective-permute-start.4 = (bf16[2,128,512]{2,1,0:T(8,128)(2,1)S(1)}, bf16[2,128,512]{2,1,0:T(8,128)(2,1)S(1)}, u32[]{:S(2)}, u32[]{:S(2)}) collective-permute-start(bf16[2,128,512]{2,1,0:T(8,128)(2,1)S(1)} %shard_map.49), channel_id=1, source_target_pairs={{0,6},{1,7},{2,4},{3,5},{4,2},{5,3},{6,0},{7,1},{8,14},{9,15},{10,... | collective-permute-start | bytes 786440 | tf_op jit(solution)/shard_map/ppermute | solution.py:274
  16.0 0.0 collective-permute-done.received
  16.0 0.1 shard_map.48
  16.1 0.1 collective-permute-start.1
  16.1 0.6 %collective-permute-start.2 = (bf16[2,128,512]{2,1,0:T(8,128)(2,1)S(1)}, bf16[2,128,512]{2,1,0:T(8,128)(2,1)S(1)}, u32[]{:S(2)}, u32[]{:S(2)}) collective-permute-start(bf16[2,128,512]{2,1,0:T(8,128)(2,1)S(1)} %get-tuple-element.31), channel_id=1, source_target_pairs={{0,2},{1,5},{2,0},{3,7},{4,6},{5,1},{6,4},{7,3},{8,10},{9,13},{10,... | collective-permute-start | bytes 786440 | tf_op jit(solution)/shard_map/ppermute | solution.py:274
  16.7 0.0 collective-permute-done.5.received
  16.7 0.1 shard_map.51
  16.8 6.3 %collective-permute-done.4.refs_3_ = bf16[2,128,512]{2,1,0:T(8,128)(2,1)S(1)} collective-permute-done((bf16[2,128,512]{2,1,0:T(8,128)(2,1)S(1)}, bf16[2,128,512]{2,1,0:T(8,128)(2,1)S(1)}, u32[]{:S(2)}, u32[]{:S(2)}) %collective-permute-start.4) | collective-permute-done | bytes 262176 | tf_op jit(solution)/shard_map/ppermute | solution.py:274
  23.2 5.4 %collective-permute-done.1.refs_1_ = bf16[2,128,512]{2,1,0:T(8,128)(2,1)S(1)} collective-permute-done((bf16[2,128,512]{2,1,0:T(8,128)(2,1)S(1)}, bf16[2,128,512]{2,1,0:T(8,128)(2,1)S(1)}, u32[]{:S(2)}, u32[]{:S(2)}) %collective-permute-start.1) | collective-permute-done | bytes 262176 | tf_op jit(solution)/shard_map/ppermute | solution.py:274
  28.5 0.1 shard_map.52.mine
  28.6 0.1 collective-permute-start.6
  28.7 0.6 %collective-permute-start.7 = (bf16[4,128,128]{2,1,0:T(8,128)(2,1)S(1)}, bf16[4,128,128]{2,1,0:T(8,128)(2,1)S(1)}, u32[]{:S(2)}, u32[]{:S(2)}) collective-permute-start(bf16[4,128,128]{2,1,0:T(8,128)(2,1)S(1)} %get-tuple-element.41), channel_id=1, source_target_pairs={{0,4},{1,3},{2,6},{3,1},{4,0},{5,7},{6,2},{7,5},{8,12},{9,11},{10,... | collective-permute-start | bytes 393224 | tf_op jit(solution)/shard_map/ppermute | solution.py:274
  29.4 2.1 %collective-permute-start.8 = (bf16[4,128,128]{2,1,0:T(8,128)(2,1)S(1)}, bf16[4,128,128]{2,1,0:T(8,128)(2,1)S(1)}, u32[]{:S(2)}, u32[]{:S(2)}) collective-permute-start(bf16[4,128,128]{2,1,0:T(8,128)(2,1)S(1)} %get-tuple-element.42), channel_id=1, source_target_pairs={{0,2},{1,5},{2,0},{3,7},{4,6},{5,1},{6,4},{7,3},{8,10},{9,13},{10,... | collective-permute-start | bytes 393224 | tf_op jit(solution)/shard_map/ppermute | solution.py:274
  31.5 0.8 %collective-permute-start.9 = (bf16[4,128,128]{2,1,0:T(8,128)(2,1)S(1)}, bf16[4,128,128]{2,1,0:T(8,128)(2,1)S(1)}, u32[]{:S(2)}, u32[]{:S(2)}) collective-permute-start(bf16[4,128,128]{2,1,0:T(8,128)(2,1)S(1)} %get-tuple-element.43), channel_id=1, source_target_pairs={{0,6},{1,7},{2,4},{3,5},{4,2},{5,3},{6,0},{7,1},{8,14},{9,15},{10,... | collective-permute-start | bytes 393224 | tf_op jit(solution)/shard_map/ppermute | solution.py:274
  32.3 0.4 shard_map.53
  32.6 1.6 %collective-permute-done.7.refs_1_ = bf16[4,128,128]{2,1,0:T(8,128)(2,1)S(1)} collective-permute-done((bf16[4,128,128]{2,1,0:T(8,128)(2,1)S(1)}, bf16[4,128,128]{2,1,0:T(8,128)(2,1)S(1)}, u32[]{:S(2)}, u32[]{:S(2)}) %collective-permute-start.7) | collective-permute-done | bytes 131104 | tf_op jit(solution)/shard_map/ppermute | solution.py:274
  34.2 1.2 %collective-permute-done.8.refs_2_ = bf16[4,128,128]{2,1,0:T(8,128)(2,1)S(1)} collective-permute-done((bf16[4,128,128]{2,1,0:T(8,128)(2,1)S(1)}, bf16[4,128,128]{2,1,0:T(8,128)(2,1)S(1)}, u32[]{:S(2)}, u32[]{:S(2)}) %collective-permute-start.8) | collective-permute-done | bytes 131104 | tf_op jit(solution)/shard_map/ppermute | solution.py:274
  35.3 2.7 %collective-permute-done.9.refs_3_ = bf16[4,128,128]{2,1,0:T(8,128)(2,1)S(1)} collective-permute-done((bf16[4,128,128]{2,1,0:T(8,128)(2,1)S(1)}, bf16[4,128,128]{2,1,0:T(8,128)(2,1)S(1)}, u32[]{:S(2)}, u32[]{:S(2)}) %collective-permute-start.9) | collective-permute-done | bytes 131104 | tf_op jit(solution)/shard_map/ppermute | solution.py:274
  38.0 1.4 %shard_map.56.refs_2_ = bf16[4,128,128]{2,1,0:T(8,128)(2,1)S(1)} custom-call(bf16[512,1024]{1,0:T(8,128)(2,1)S(1)} %get-tuple-element.39.system, bf16[512,512]{1,0:T(8,128)(2,1)S(1)} %get-tuple-element.40.rough, f32[512,128]{1,0:T(8,128)S(1)} %get-tuple-element.37.refs_0_.diag_sum, bf16[4,128,128]{2,1,0:T(8,128)(2,1)S(1)} %get-tuple-element.36.refs_4_.refs_0_, ...), custom_call_target="tpu_custom_call" | custom-call | flops 805306368 | bytes 2097152 | tf_op jit(solution)/shard_map/pallas_call | solution.py:364
  39.4 0.1 collective-permute-start.15
  39.5 1.4 %shard_map.58.refs_0_ = bf16[768,256]{1,0:T(8,128)(2,1)S(1)} custom-call(bf16[4,6,24,128]{3,2,1,0:T(8,128)(2,1)S(1)} %broadcast_in_dim.2.mask, bf16[4,6,24,128,128]{4,3,2,1,0:T(8,128)(2,1)S(1)} %copy-done, bf16[3072,256]{1,0:T(8,128)(2,1)S(1)} %copy-done.2), custom_call_target="tpu_custom_call" | custom-call | flops 1207959552 | bytes 6291456 | tf_op jit(solution)/shard_map/pallas_call | solution.py:332
  40.9 2.1 %collective-permute-start.14 = (bf16[4,128,128]{2,1,0:T(8,128)(2,1)S(1)}, bf16[4,128,128]{2,1,0:T(8,128)(2,1)S(1)}, u32[]{:S(2)}, u32[]{:S(2)}) collective-permute-start(bf16[4,128,128]{2,1,0:T(8,128)(2,1)S(1)} %shard_map.56.refs_2_), channel_id=1, source_target_pairs={{0,6},{1,7},{2,4},{3,5},{4,2},{5,3},{6,0},{7,1},{8,14},{9,15},{10,... | collective-permute-start | bytes 393224 | tf_op jit(solution)/shard_map/ppermute | solution.py:274
  43.0 0.3 collective-permute-start.11
  43.3 1.1 %collective-permute-start.10 = (bf16[4,128,128]{2,1,0:T(8,128)(2,1)S(1)}, bf16[4,128,128]{2,1,0:T(8,128)(2,1)S(1)}, u32[]{:S(2)}, u32[]{:S(2)}) collective-permute-start(bf16[4,128,128]{2,1,0:T(8,128)(2,1)S(1)} %shard_map.56.refs_2_), channel_id=1, source_target_pairs={{0,4},{1,3},{2,6},{3,1},{4,0},{5,7},{6,2},{7,5},{8,12},{9,11},{10,... | collective-permute-start | bytes 393224 | tf_op jit(solution)/shard_map/ppermute | solution.py:274
  44.4 1.4 %shard_map.54.order_only.refs_0_ = bf16[768,256]{1,0:T(8,128)(2,1)S(1)} custom-call(bf16[4,6,24,128]{3,2,1,0:T(8,128)(2,1)S(1)} %broadcast_in_dim.2.mask, bf16[4,6,24,128,128]{4,3,2,1,0:T(8,128)(2,1)S(1)} %copy-done, bf16[3072,256]{1,0:T(8,128)(2,1)S(1)} %copy-done.2, f32[512,128]{1,0:T(8,128)S(1)} %get-tuple-element.37.refs_0_.diag_sum), custom_call_target="tpu_custom_call" | custom-call | flops 1207959552 | bytes 6291456 | tf_op jit(solution)/shard_map/pallas_call | solution.py:332
  45.8 1.5 %shard_map.55 = (bf16[768,512]{1,0:T(8,128)(2,1)S(1)}, bf16[768,512]{1,0:T(8,128)(2,1)S(1)}, bf16[768,512]{1,0:T(8,128)(2,1)S(1)}, bf16[768,512]{1,0:T(8,128)(2,1)S(1)}) custom-call(s32[4,4]{1,0:T(4,128)S(1)} %copy-done.4, s32[6,4,24]{2,1,0:T(4,128)S(1)} %bitcast.2, bf16[4,6,24,128,128]{4,3,2,1,0:T(8,128)(2,1)S(1)} %copy-done, ...), custom_call_target="tpu_custom_call" | custom-call | bytes 6291456 | tf_op jit(solution)/shard_map/pallas_call | solution.py:359
  47.3 0.0 collective-permute-done.15.refs_3_
  47.3 1.1 %shard_map.59.refs_4_ = bf16[4,768,256]{2,1,0:T(8,128)(2,1)} custom-call(bf16[768,256]{1,0:T(8,128)(2,1)S(1)} %shard_map.58.refs_0_, bf16[768,512]{1,0:T(8,128)(2,1)S(1)} %get-tuple-element.46.refs_1_, bf16[4,128,128]{2,1,0:T(8,128)(2,1)S(1)} %shard_map.56.refs_2_, bf16[4,128,128]{2,1,0:T(8,128)(2,1)S(1)} %collective-permute-done.15.refs_3_), custom_call_target="tpu_custom_call" | custom-call | flops 201326592 | bytes 2097152 | tf_op jit(solution)/shard_map/pallas_call | solution.py:381
  48.5 0.1 collective-permute-start.16
  48.6 1.4 %shard_map.46.refs_0_ = bf16[768,256]{1,0:T(8,128)(2,1)S(1)} custom-call(bf16[4,6,24,128]{3,2,1,0:T(8,128)(2,1)S(1)} %broadcast_in_dim.2.mask, bf16[4,6,24,128,128]{4,3,2,1,0:T(8,128)(2,1)S(1)} %copy-done, bf16[3072,256]{1,0:T(8,128)(2,1)S(1)} %copy-done.2), custom_call_target="tpu_custom_call" | custom-call | flops 1207959552 | bytes 6291456 | tf_op jit(solution)/shard_map/pallas_call | solution.py:332
  50.0 0.0 collective-permute-done.11.refs_6_
  50.0 0.6 %collective-permute-start.12 = (bf16[4,128,128]{2,1,0:T(8,128)(2,1)S(1)}, bf16[4,128,128]{2,1,0:T(8,128)(2,1)S(1)}, u32[]{:S(2)}, u32[]{:S(2)}) collective-permute-start(bf16[4,128,128]{2,1,0:T(8,128)(2,1)S(1)} %collective-permute-done.11.refs_6_), channel_id=1, source_target_pairs={{0,1},{1,0},{2,3},{3,2},{4,5},{5,4},{6,7},{7,6},{8,9},{9,8},{10,11... | collective-permute-start | bytes 393224 | tf_op jit(solution)/shard_map/ppermute | solution.py:265
  50.6 0.0 collective-permute-done.10.refs_2_
  50.6 0.1 collective-permute-start.13
  50.6 1.4 %shard_map.57.refs_4_ = bf16[768,256]{1,0:T(8,128)(2,1)S(1)} custom-call(bf16[4,6,24,128]{3,2,1,0:T(8,128)(2,1)S(1)} %broadcast_in_dim.2.mask, bf16[4,6,24,128,128]{4,3,2,1,0:T(8,128)(2,1)S(1)} %copy-done, bf16[3072,256]{1,0:T(8,128)(2,1)S(1)} %copy-done.2), custom_call_target="tpu_custom_call" | custom-call | flops 1207959552 | bytes 6291456 | tf_op jit(solution)/shard_map/pallas_call | solution.py:332
  52.0 1.1 %shard_map.60.refs_8_ = bf16[4,768,256]{2,1,0:T(8,128)(2,1)} custom-call(bf16[768,256]{1,0:T(8,128)(2,1)S(1)} %shard_map.54.order_only.refs_0_, bf16[768,512]{1,0:T(8,128)(2,1)S(1)} %get-tuple-element.45.refs_1_, bf16[4,128,128]{2,1,0:T(8,128)(2,1)S(1)} %collective-permute-done.14.refs_2_, ...), custom_call_target="tpu_custom_call", output_to_operand_aliasing={{}: (4, {})} | custom-call | flops 201326592 | bytes 2097152 | tf_op jit(solution)/shard_map/pallas_call | solution.py:381
  53.2 0.0 collective-permute-done.12.refs_3_
  53.2 1.5 %shard_map.61 = bf16[4,768,256]{2,1,0:T(8,128)(2,1)} custom-call(bf16[768,256]{1,0:T(8,128)(2,1)S(1)} %shard_map.46.refs_0_, bf16[768,512]{1,0:T(8,128)(2,1)S(1)} %get-tuple-element.38.refs_1_, bf16[4,128,128]{2,1,0:T(8,128)(2,1)S(1)} %collective-permute-done.10.refs_2_, ...), custom_call_target="tpu_custom_call", output_to_operand_aliasing={{}: (8, {})} | custom-call | flops 402653184 | bytes 4194304 | tf_op jit(solution)/shard_map/pallas_call | solution.py:381
  (16 shorter events, 0.1 us)
Async XLA Ops:
  0.0 3.2 %copy-start.4 = (s32[4,4]{1,0:T(4,128)S(1)}, s32[4,4]{1,0:T(4,128)}, u32[]{:S(2)}) copy-start(s32[4,4]{1,0:T(4,128)} %shared.5) | copy-start | bytes 196
  0.0 3.3 %copy-start.3 = (s32[4,6,24]{2,0,1:T(4,128)S(1)}, s32[4,6,24]{2,0,1:T(4,128)}, u32[]{:S(2)}) copy-start(s32[4,6,24]{2,0,1:T(4,128)} %param.5) | copy-start | bytes 6916
  0.0 6.6 %copy-start = (bf16[4,6,24,128,128]{4,3,2,1,0:T(8,128)(2,1)S(1)}, bf16[4,6,24,128,128]{4,3,2,1,0:T(8,128)(2,1)}, u32[]{:S(2)}) copy-start(bf16[4,6,24,128,128]{4,3,2,1,0:T(8,128)(2,1)} %blocks.13) | copy-start | bytes 56623108
  2.6 13.3 %collective-permute-start = (bf16[3,2,128,512]{3,2,1,0:T(8,128)(2,1)S(1)}, bf16[3,2,128,512]{3,2,1,0:T(8,128)(2,1)S(1)}, u32[]{:S(2)}, u32[]{:S(2)}) collective-permute-start(bf16[3,2,128,512]{3,2,1,0:T(8,128)(2,1)S(1)} %get-tuple-element.28), channel_id=1, source_target_pairs={{0,1},{1,0},{2,3},{3,2},{4,5},{5,4},{6,7},{7,6},{8,9},{9,8},{10,11... | collective-permute-start | bytes 2359304 | tf_op jit(solution)/shard_map/ppermute | solution.py:265
  2.9 7.8 %collective-permute-start.3 = (bf16[1,2,128,512]{3,2,1,0:T(8,128)(2,1)S(1)}, bf16[1,2,128,512]{3,2,1,0:T(8,128)(2,1)S(1)}, u32[]{:S(2)}, u32[]{:S(2)}) collective-permute-start(bf16[1,2,128,512]{3,2,1,0:T(8,128)(2,1)S(1)} %get-tuple-element.33), channel_id=1, source_target_pairs={{0,1},{1,0},{2,3},{3,2},{4,5},{5,4},{6,7},{7,6},{8,9},{9,8},{10,11... | collective-permute-start | bytes 786440 | tf_op jit(solution)/shard_map/ppermute | solution.py:265
  6.6 1.4 %copy-start.1 = (bf16[3072,256]{1,0:T(8,128)(2,1)S(1)}, bf16[3072,256]{1,0:T(8,128)(2,1)}, u32[]{:S(2)}) copy-start(bf16[3072,256]{1,0:T(8,128)(2,1)} %sketch.9) | copy-start | bytes 4718596
  10.6 6.1 %collective-permute-start.5 = (bf16[4,4,128,128]{3,2,1,0:T(8,128)(2,1)S(1)}, bf16[4,4,128,128]{3,2,1,0:T(8,128)(2,1)S(1)}, u32[]{:S(2)}, u32[]{:S(2)}) collective-permute-start(bf16[4,4,128,128]{3,2,1,0:T(8,128)(2,1)S(1)} %get-tuple-element.35), channel_id=1, source_target_pairs={{0,1},{1,0},{2,3},{3,2},{4,5},{5,4},{6,7},{7,6},{8,9},{9,8},{10,11... | collective-permute-start | bytes 1572872 | tf_op jit(solution)/shard_map/ppermute | solution.py:265
  10.8 12.4 %collective-permute-start.4 = (bf16[2,128,512]{2,1,0:T(8,128)(2,1)S(1)}, bf16[2,128,512]{2,1,0:T(8,128)(2,1)S(1)}, u32[]{:S(2)}, u32[]{:S(2)}) collective-permute-start(bf16[2,128,512]{2,1,0:T(8,128)(2,1)S(1)} %shard_map.49), channel_id=1, source_target_pairs={{0,6},{1,7},{2,4},{3,5},{4,2},{5,3},{6,0},{7,1},{8,14},{9,15},{10,... | collective-permute-start | bytes 786440 | tf_op jit(solution)/shard_map/ppermute | solution.py:274
  16.1 12.5 %collective-permute-start.1 = (bf16[2,128,512]{2,1,0:T(8,128)(2,1)S(1)}, bf16[2,128,512]{2,1,0:T(8,128)(2,1)S(1)}, u32[]{:S(2)}, u32[]{:S(2)}) collective-permute-start(bf16[2,128,512]{2,1,0:T(8,128)(2,1)S(1)} %get-tuple-element.30), channel_id=1, source_target_pairs={{0,4},{1,3},{2,6},{3,1},{4,0},{5,7},{6,2},{7,5},{8,12},{9,11},{10,... | collective-permute-start | bytes 786440 | tf_op jit(solution)/shard_map/ppermute | solution.py:274
  16.1 12.4 %collective-permute-start.2 = (bf16[2,128,512]{2,1,0:T(8,128)(2,1)S(1)}, bf16[2,128,512]{2,1,0:T(8,128)(2,1)S(1)}, u32[]{:S(2)}, u32[]{:S(2)}) collective-permute-start(bf16[2,128,512]{2,1,0:T(8,128)(2,1)S(1)} %get-tuple-element.31), channel_id=1, source_target_pairs={{0,2},{1,5},{2,0},{3,7},{4,6},{5,1},{6,4},{7,3},{8,10},{9,13},{10,... | collective-permute-start | bytes 786440 | tf_op jit(solution)/shard_map/ppermute | solution.py:274
  28.6 3.6 %collective-permute-start.6 = (bf16[2,2,128,512]{3,2,1,0:T(8,128)(2,1)S(1)}, bf16[2,2,128,512]{3,2,1,0:T(8,128)(2,1)S(1)}, u32[]{:S(2)}, u32[]{:S(2)}) collective-permute-start(bf16[2,2,128,512]{3,2,1,0:T(8,128)(2,1)S(1)} %shard_map.52.mine), channel_id=1, source_target_pairs={{0,1},{1,0},{2,3},{3,2},{4,5},{5,4},{6,7},{7,6},{8,9},{9,8},{10,11... | collective-permute-start | bytes 1572872 | tf_op jit(solution)/shard_map/ppermute | solution.py:265
  28.7 5.4 %collective-permute-start.7 = (bf16[4,128,128]{2,1,0:T(8,128)(2,1)S(1)}, bf16[4,128,128]{2,1,0:T(8,128)(2,1)S(1)}, u32[]{:S(2)}, u32[]{:S(2)}) collective-permute-start(bf16[4,128,128]{2,1,0:T(8,128)(2,1)S(1)} %get-tuple-element.41), channel_id=1, source_target_pairs={{0,4},{1,3},{2,6},{3,1},{4,0},{5,7},{6,2},{7,5},{8,12},{9,11},{10,... | collective-permute-start | bytes 393224 | tf_op jit(solution)/shard_map/ppermute | solution.py:274
  29.4 6.0 %collective-permute-start.8 = (bf16[4,128,128]{2,1,0:T(8,128)(2,1)S(1)}, bf16[4,128,128]{2,1,0:T(8,128)(2,1)S(1)}, u32[]{:S(2)}, u32[]{:S(2)}) collective-permute-start(bf16[4,128,128]{2,1,0:T(8,128)(2,1)S(1)} %get-tuple-element.42), channel_id=1, source_target_pairs={{0,2},{1,5},{2,0},{3,7},{4,6},{5,1},{6,4},{7,3},{8,10},{9,13},{10,... | collective-permute-start | bytes 393224 | tf_op jit(solution)/shard_map/ppermute | solution.py:274
  31.5 6.5 %collective-permute-start.9 = (bf16[4,128,128]{2,1,0:T(8,128)(2,1)S(1)}, bf16[4,128,128]{2,1,0:T(8,128)(2,1)S(1)}, u32[]{:S(2)}, u32[]{:S(2)}) collective-permute-start(bf16[4,128,128]{2,1,0:T(8,128)(2,1)S(1)} %get-tuple-element.43), channel_id=1, source_target_pairs={{0,6},{1,7},{2,4},{3,5},{4,2},{5,3},{6,0},{7,1},{8,14},{9,15},{10,... | collective-permute-start | bytes 393224 | tf_op jit(solution)/shard_map/ppermute | solution.py:274
  32.6 6.8 %copy-start.2 = (bf16[3072,256]{1,0:T(8,128)(2,1)S(1)}, bf16[3072,256]{1,0:T(8,128)(2,1)}, u32[]{:S(2)}) copy-start(bf16[3072,256]{1,0:T(8,128)(2,1)} %sketch.9) | copy-start | bytes 4718596
  39.4 7.9 %collective-permute-start.15 = (bf16[4,128,128]{2,1,0:T(8,128)(2,1)S(1)}, bf16[4,128,128]{2,1,0:T(8,128)(2,1)S(1)}, u32[]{:S(2)}, u32[]{:S(2)}) collective-permute-start(bf16[4,128,128]{2,1,0:T(8,128)(2,1)S(1)} %shard_map.56.refs_2_), channel_id=1, source_target_pairs={{0,1},{1,0},{2,3},{3,2},{4,5},{5,4},{6,7},{7,6},{8,9},{9,8},{10,11... | collective-permute-start | bytes 393224 | tf_op jit(solution)/shard_map/ppermute | solution.py:265
  40.9 7.6 %collective-permute-start.14 = (bf16[4,128,128]{2,1,0:T(8,128)(2,1)S(1)}, bf16[4,128,128]{2,1,0:T(8,128)(2,1)S(1)}, u32[]{:S(2)}, u32[]{:S(2)}) collective-permute-start(bf16[4,128,128]{2,1,0:T(8,128)(2,1)S(1)} %shard_map.56.refs_2_), channel_id=1, source_target_pairs={{0,6},{1,7},{2,4},{3,5},{4,2},{5,3},{6,0},{7,1},{8,14},{9,15},{10,... | collective-permute-start | bytes 393224 | tf_op jit(solution)/shard_map/ppermute | solution.py:274
  43.0 7.0 %collective-permute-start.11 = (bf16[4,128,128]{2,1,0:T(8,128)(2,1)S(1)}, bf16[4,128,128]{2,1,0:T(8,128)(2,1)S(1)}, u32[]{:S(2)}, u32[]{:S(2)}) collective-permute-start(bf16[4,128,128]{2,1,0:T(8,128)(2,1)S(1)} %shard_map.56.refs_2_), channel_id=1, source_target_pairs={{0,2},{1,5},{2,0},{3,7},{4,6},{5,1},{6,4},{7,3},{8,10},{9,13},{10,... | collective-permute-start | bytes 393224 | tf_op jit(solution)/shard_map/ppermute | solution.py:274
  43.3 7.2 %collective-permute-start.10 = (bf16[4,128,128]{2,1,0:T(8,128)(2,1)S(1)}, bf16[4,128,128]{2,1,0:T(8,128)(2,1)S(1)}, u32[]{:S(2)}, u32[]{:S(2)}) collective-permute-start(bf16[4,128,128]{2,1,0:T(8,128)(2,1)S(1)} %shard_map.56.refs_2_), channel_id=1, source_target_pairs={{0,4},{1,3},{2,6},{3,1},{4,0},{5,7},{6,2},{7,5},{8,12},{9,11},{10,... | collective-permute-start | bytes 393224 | tf_op jit(solution)/shard_map/ppermute | solution.py:274
  48.5 3.5 %collective-permute-start.16 = (bf16[4,128,128]{2,1,0:T(8,128)(2,1)S(1)}, bf16[4,128,128]{2,1,0:T(8,128)(2,1)S(1)}, u32[]{:S(2)}, u32[]{:S(2)}) collective-permute-start(bf16[4,128,128]{2,1,0:T(8,128)(2,1)S(1)} %collective-permute-done.14.refs_2_), channel_id=1, source_target_pairs={{0,1},{1,0},{2,3},{3,2},{4,5},{5,4},{6,7},{7,6},{8,9},{9,8},{10,11... | collective-permute-start | bytes 393224 | tf_op jit(solution)/shard_map/ppermute | solution.py:265
  50.0 3.2 %collective-permute-start.12 = (bf16[4,128,128]{2,1,0:T(8,128)(2,1)S(1)}, bf16[4,128,128]{2,1,0:T(8,128)(2,1)S(1)}, u32[]{:S(2)}, u32[]{:S(2)}) collective-permute-start(bf16[4,128,128]{2,1,0:T(8,128)(2,1)S(1)} %collective-permute-done.11.refs_6_), channel_id=1, source_target_pairs={{0,1},{1,0},{2,3},{3,2},{4,5},{5,4},{6,7},{7,6},{8,9},{9,8},{10,11... | collective-permute-start | bytes 393224 | tf_op jit(solution)/shard_map/ppermute | solution.py:265
  50.6 2.6 %collective-permute-start.13 = (bf16[4,128,128]{2,1,0:T(8,128)(2,1)S(1)}, bf16[4,128,128]{2,1,0:T(8,128)(2,1)S(1)}, u32[]{:S(2)}, u32[]{:S(2)}) collective-permute-start(bf16[4,128,128]{2,1,0:T(8,128)(2,1)S(1)} %collective-permute-done.10.refs_2_), channel_id=1, source_target_pairs={{0,1},{1,0},{2,3},{3,2},{4,5},{5,4},{6,7},{7,6},{8,9},{9,8},{10,11... | collective-permute-start | bytes 393224 | tf_op jit(solution)/shard_map/ppermute | solution.py:265

commit v2 on v1

--- a/solution.py
+++ b/solution.py
@@ -33,16 +33,8 @@
     return lax.rem(face, 2), lax.bitwise_or(lax.shift_left(lax.div(face, 2), 1), lax.rem(box, 2))
 
 
-def swapped(step):
-    return (step & ~3) | ((step & 1) << 1) | ((step >> 1) & 1)
-
-
-def distance_of(step):
-    return jnp.where(place()[0] == 0, step, swapped(step))
-
-
 def box_at(step, boxes):
-    return lax.rem(lax.bitwise_xor(place()[1], distance_of(step)), boxes)
+    return lax.rem(lax.bitwise_xor(place()[1], step), boxes)
 
 
 def gather_kernel(groups, shared, pattern_hbm, blocks, *refs):
@@ -51,14 +43,14 @@
     boxes, row_count = blocks.shape[:2]
     slots = 2 * half
     row_start = lax.axis_index("face") * row_count
-    core, chip = place()
+    core = place()[0]
 
     def each(action):
         copied = 0
         for order, group in enumerate(groups):
             for where, target in ((1 - core, outs[2 * order]), (core, outs[2 * order + 1])):
-                for index, distance in enumerate(group):
-                    box = lax.rem(lax.bitwise_xor(chip, distance), boxes)
+                for index, step in enumerate(group):
+                    box = box_at(step, boxes)
                     for part in range(half):
                         slot = where * half + part
                         row = shared[box, slot] - row_start
@@ -105,24 +97,14 @@
 
 def side_sum_kernel(*refs):
     ins, out = refs[:-2], refs[-1]
-    first = place()[0] == 0
-    totals = [None, None]
-
-    def add(side, value):
-        totals[side] = value if totals[side] is None else totals[side] + value
-
-    for step, ref in enumerate(ins):
-        other = swapped(step)
-        if other == step:
-            add(step & 1, ref[...])
-        elif step & 1:
-            add(1, jnp.where(first, ref[...], ins[other][...]))
-            add(0, jnp.where(first, ins[other][...], ref[...]))
-    for side, total in enumerate(totals):
+    for side in range(2):
+        total = ins[side][...]
+        for ref in ins[side + 2 :: 2]:
+            total = total + ref[...]
         out[side] = total
 
 
-def system_kernel(mine, theirs, system, rough, diag_sum):
+def system_kernel(mine, theirs, system, rough, inverse):
     _, half, blk, width = mine.shape
     slots = 2 * half
     core = place()[0]
@@ -139,7 +121,7 @@
             rows, width + slot * blk : width + (slot + 1) * blk
         ].astype(jnp.float32)
         line = jnp.sum(jnp.where(eye, both, 0.0), axis=1, keepdims=True)
-        diag_sum[rows, :] = jnp.broadcast_to(line, (blk, diag_sum.shape[1]))
+        inverse[rows, :] = jnp.broadcast_to(1.0 / line, (blk, inverse.shape[1]))
         rough[rows, rows] = jnp.where(eye, 0.0, both).astype(rough.dtype)
 
 
@@ -203,26 +185,26 @@
                 )
 
 
-def solve_kernel(system, rough, diag_sum, *refs):
+def solve_kernel(system, rough, inverse, *refs):
     rhs_refs, out = refs[:-1], refs[-1]
     right_side = rhs_refs[0][...].astype(jnp.float32)
     for ref in rhs_refs[1:]:
         right_side = right_side + ref[...].astype(jnp.float32)
     slots, blk, cols = right_side.shape
     right_side = right_side.reshape(slots * blk, cols)
-    potential = right_side / diag_sum[...]
+    potential = right_side * inverse[...]
     for sweep in range(ITERS - 1):
         high = potential.astype(jnp.bfloat16)
         low = (potential - high.astype(jnp.float32)).astype(jnp.bfloat16)
         both = jnp.concatenate([high, low], axis=1)
         if sweep < ITERS - 2:
             applied = jnp.dot(rough[...], both, preferred_element_type=jnp.float32)
-            potential = (right_side - applied[:, :cols] - applied[:, cols:]) / diag_sum[...]
+            potential = (right_side - applied[:, :cols] - applied[:, cols:]) * inverse[...]
         else:
             stacked = jnp.concatenate([both, both], axis=0)
             applied = jnp.dot(system[...], stacked, preferred_element_type=jnp.float32)
             applied = applied[:, :cols] + applied[:, cols:]
-            potential = potential + (right_side - applied) / diag_sum[...]
+            potential = potential + (right_side - applied) * inverse[...]
     out[...] = potential.astype(out.dtype).reshape(out.shape)
 
 
@@ -238,11 +220,17 @@
         other = theirs[...].reshape(slots * blk, cols)
         parts = [jnp.where(core == 0, own, other), jnp.where(core == 0, other, own)]
         potential = jnp.concatenate(parts, axis=1)
-        correction = jnp.dot(side[...], potential, preferred_element_type=jnp.float32)
-        result[index] = (sketched[...].astype(jnp.float32) - correction).astype(result.dtype)
-        copy = pltpu.make_async_copy(result.at[index], out.at[box_at(step, boxes)], sems.at[index])
-        copy.start()
-        copies.append(copy)
+        pieces = sems.shape[0] // len(steps)
+        piece = sketched.shape[0] // pieces
+        for part in range(pieces):
+            rows = pl.ds(part * piece, piece)
+            correction = jnp.dot(side[rows], potential, preferred_element_type=jnp.float32)
+            result[index, rows] = (sketched[rows].astype(jnp.float32) - correction).astype(result.dtype)
+            copy = pltpu.make_async_copy(
+                result.at[index, rows], out.at[box_at(step, boxes), rows], sems.at[index * pieces + part]
+            )
+            copy.start()
+            copies.append(copy)
     for copy in copies:
         copy.wait()
 
@@ -268,8 +256,7 @@
         pairs = []
         for b in range(box_size):
             for f in range(face_size):
-                distance = swapped(step) if f & 1 else step
-                target = (b ^ (distance & 1)) * face_size + (f ^ (2 * (distance >> 1)))
+                target = (b ^ (step & 1)) * face_size + (f ^ (2 * (step >> 1)))
                 pairs.append((b * face_size + f, target))
         return lax.ppermute(value, ("box", "face"), pairs)
 
@@ -315,7 +302,7 @@
             last_steps,
             merged(
                 keep_late, other_core(send_late), last_steps,
-                lambda s: lax.rem(distance_of(s), boxes),
+                lambda s: late.index(s % boxes),
             ),
         )
     )
@@ -342,10 +329,8 @@
     arrived_y = around(outs_y)
 
     both_shape = jax.ShapeDtypeStruct((2,) + outs[0].shape, kind)
-    mine = call(
-        side_sum_kernel, both_shape, 4, [VMEM] * chips + [ANY], VMEM, moved=3 * MIB // 2
-    )(*arrived, outs_y[0])
-    system, rough, diag_sum = call(
+    mine = call(side_sum_kernel, both_shape, 4, [VMEM] * chips + [ANY], VMEM, moved=3 * MIB // 2)(*arrived, outs_y[0])
+    system, rough, inverse = call(
         system_kernel,
         [
             jax.ShapeDtypeStruct((slots * blk, 2 * slots * blk), kind),
@@ -355,7 +340,7 @@
         6, [VMEM] * 2, [VMEM] * 3, moved=2 * MIB,
     )(mine, other_core(mine))
 
-    sketches = [sketch_at(s) for s in range(boxes - 1)] + [sketch_at(boxes - 1, diag_sum)]
+    sketches = [sketch_at(s) for s in range(boxes)]
     sides = call(
         side_kernel, [jax.ShapeDtypeStruct((order, slots * blk), kind)] * boxes, 6,
         [SMEM, SMEM, VMEM, ANY], [VMEM] * boxes, moved=6 * MIB,
@@ -366,17 +351,18 @@
         jax.ShapeDtypeStruct((slots, blk, cols // 2), kind), 8,
         [VMEM] * (3 + chips), VMEM,
         flops=2 * (ITERS - 1) * 2 * (slots * blk) ** 2 * cols, moved=2 * MIB,
-    )(system, rough, diag_sum, *arrived_y)
+    )(system, rough, inverse, *arrived_y)
 
     back = around([potential] * boxes)
     out_shape = jax.ShapeDtypeStruct((boxes, order, cols), kind)
     theirs = [None] * boxes
     result = []
+    pieces = 3 if row_count % 3 == 0 else 1
 
     def correct(*steps):
         inputs = []
         for s in steps:
-            inputs += [sketches[s], sides[s], back[s], theirs[swapped(s)]]
+            inputs += [sketches[s], sides[s], back[s], theirs[s]]
         count = len(inputs)
         corrected = call(
             functools.partial(correct_kernel, steps), out_shape, 2 + 2 * len(steps),
@@ -384,7 +370,7 @@
             flops=2 * len(steps) * order * slots * blk * cols, moved=2 * len(steps) * MIB,
             scratch_shapes=[
                 pltpu.VMEM((len(steps), order, cols), kind),
-                pltpu.SemaphoreType.DMA((len(steps),)),
+                pltpu.SemaphoreType.DMA((pieces * len(steps),)),
             ],
             input_output_aliases={count: 0} if result else {},
         )(*inputs, *result)

time: 54.9 us -> 57.2 us (1.042)
  waiting for transfers between devices: 17.1 us -> 20.3 us
  starting transfers between devices: 14.5 us -> 13.9 us
    ppermute x9, waiting for transfers between devices: 17.1 us -> 20.2 us  [chip_at(): return lax.ppermute(value, ('box', 'face'), pairs)]
    ppermute x8, starting transfers between devices: 1.58 us -> 0.99 us  [other_core(): return lax.ppermute(value, 'face', pairs)]
  transfers between devices with their start and end apart: 17 -> 17, of which waited for: 5 -> 8; matrix products, arithmetic and copies ran while one was open for 0% -> 0% of each run, Pallas kernels for 23% -> 22%
where the time goes in v2:
time: 57.2 us; the launch traced here: 57 us
  waiting for transfers between devices  20.3 us (35%)
  Pallas kernels  17.8 us (31%)
  starting transfers between devices  13.9 us (24%)
  local copies, waits for them, and re-layouts  4.72 us (8%)
    ppermute x9, waiting for transfers between devices, chip_at(): return lax.ppermute(value, ('box', 'face'), pairs)  20.2 us
    ppermute x9, starting transfers between devices, chip_at(): return lax.ppermute(value, ('box', 'face'), pairs)  13 us
    pallas_call x4, Pallas kernels, sketch_at(): call(functools.partial(sketch_kernel, step), jax.ShapeDtypeStruct((order,...  5.56 us
    unnamed x10, local copies, waits for them, and re-layouts  4.57 us
    pallas_call x3, Pallas kernels, correct(): call(functools.partial(correct_kernel, steps), out_shape, 2 + 2 * len(ste...  3.57 us
    pallas_call x1, Pallas kernels, local(): call(functools.partial(gather_kernel, (early, late)), part_shapes, 4, [SM...  2.63 us
    pallas_call x1, Pallas kernels, local(): call(right_kernel, [half_shape] * 2, 6, [SMEM] + [VMEM] * 3, [VMEM] * 2,...  2.58 us
    pallas_call x1, Pallas kernels, local(): call(side_kernel, [jax.ShapeDtypeStruct((order, slots * blk), kind)] * bo...  1.46 us
  transfers between devices with their start and end apart: 17, of which 8 were waited for; matrix products, arithmetic and copies ran while one was open for 0% of the time, Pallas kernels for 22%

profile of v2, /device:TPU:0, one launch (start us, length us, event | category | flops | bytes accessed | tf_op | source)
XLA Modules:
  0.0 57.0 jit_solution(772568206519518260)
XLA Ops:
  0.0 2.6 %shard_map.49 = (bf16[1,2,128,512]{3,2,1,0:T(8,128)(2,1)S(1)}, bf16[1,2,128,512]{3,2,1,0:T(8,128)(2,1)S(1)}, bf16[3,2,128,512]{3,2,1,0:T(8,128)(2,1)S(1)}, bf16[3,2,128,512]{3,2,1,0:T(8,128)(2,1)S(1)}) custom-call(s32[4,4]{1,0:T(4,128)} %shared.5, s32[6,4,24]{2,1,0:T(4,128)} %bitcast.1, bf16[4,6,24,128,128]{4,3,2,1,0:T(8,128)(2,1)} %blocks.13), custom_call_target="tpu_custom_call" | custom-call | bytes 2097152 | tf_op jit(solution)/shard_map/pallas_call | solution.py:281
  2.6 0.3 collective-permute-start
  2.9 0.3 collective-permute-start.3
  3.2 0.1 fusion
  3.4 0.1 broadcast_in_dim.2.mask
  3.5 3.2 %copy-done = bf16[4,6,24,128,128]{4,3,2,1,0:T(8,128)(2,1)S(1)} copy-done((bf16[4,6,24,128,128]{4,3,2,1,0:T(8,128)(2,1)S(1)}, bf16[4,6,24,128,128]{4,3,2,1,0:T(8,128)(2,1)}, u32[]{:S(2)}) %copy-start) | copy-done | bytes 18874392
  6.7 1.4 %copy-done.1 = bf16[3072,256]{1,0:T(8,128)(2,1)S(1)} copy-done((bf16[3072,256]{1,0:T(8,128)(2,1)S(1)}, bf16[3072,256]{1,0:T(8,128)(2,1)}, u32[]{:S(2)}) %copy-start.1) | copy-done | bytes 1572888
  8.1 2.6 %shard_map.52 = (bf16[4,4,128,128]{3,2,1,0:T(8,128)(2,1)S(1)}, bf16[4,4,128,128]{3,2,1,0:T(8,128)(2,1)S(1)}) custom-call(s32[4,4]{1,0:T(4,128)S(1)} %copy-done.4, bf16[4,6,24,128]{3,2,1,0:T(8,128)(2,1)S(1)} %broadcast_in_dim.2.mask, bf16[4,6,24,128,128]{4,3,2,1,0:T(8,128)(2,1)S(1)} %copy-done, bf16[3072,256]{1,0:T(8,128)(2,1)S(1)} %copy-done.1), custom_call_target="tpu_custom_call" | custom-call | flops 805306368 | bytes 4194304 | tf_op jit(solution)/shard_map/pallas_call | solution.py:313
  10.6 0.1 collective-permute-start.5
  10.8 5.2 %collective-permute-start.4 = (bf16[2,128,512]{2,1,0:T(8,128)(2,1)S(1)}, bf16[2,128,512]{2,1,0:T(8,128)(2,1)S(1)}, u32[]{:S(2)}, u32[]{:S(2)}) collective-permute-start(bf16[2,128,512]{2,1,0:T(8,128)(2,1)S(1)} %shard_map.51), channel_id=1, source_target_pairs={{0,6},{1,7},{2,4},{3,5},{4,2},{5,3},{6,0},{7,1},{8,14},{9,15},{10,... | collective-permute-start | bytes 786440 | tf_op jit(solution)/shard_map/ppermute | solution.py:261
  16.0 0.1 shard_map.50
  16.1 0.1 collective-permute-start.1
  16.1 0.6 %collective-permute-start.2 = (bf16[2,128,512]{2,1,0:T(8,128)(2,1)S(1)}, bf16[2,128,512]{2,1,0:T(8,128)(2,1)S(1)}, u32[]{:S(2)}, u32[]{:S(2)}) collective-permute-start(bf16[2,128,512]{2,1,0:T(8,128)(2,1)S(1)} %get-tuple-element.32), channel_id=1, source_target_pairs={{0,2},{1,3},{2,0},{3,1},{4,6},{5,7},{6,4},{7,5},{8,10},{9,11},{10,... | collective-permute-start | bytes 786440 | tf_op jit(solution)/shard_map/ppermute | solution.py:261
  16.7 0.0 collective-permute-done.5.received
  16.7 0.1 shard_map.53
  16.8 6.3 %collective-permute-done.4.refs_3_ = bf16[2,128,512]{2,1,0:T(8,128)(2,1)S(1)} collective-permute-done((bf16[2,128,512]{2,1,0:T(8,128)(2,1)S(1)}, bf16[2,128,512]{2,1,0:T(8,128)(2,1)S(1)}, u32[]{:S(2)}, u32[]{:S(2)}) %collective-permute-start.4) | collective-permute-done | bytes 262176 | tf_op jit(solution)/shard_map/ppermute | solution.py:261
  23.2 5.4 %collective-permute-done.1.refs_1_ = bf16[2,128,512]{2,1,0:T(8,128)(2,1)S(1)} collective-permute-done((bf16[2,128,512]{2,1,0:T(8,128)(2,1)S(1)}, bf16[2,128,512]{2,1,0:T(8,128)(2,1)S(1)}, u32[]{:S(2)}, u32[]{:S(2)}) %collective-permute-start.1) | collective-permute-done | bytes 262176 | tf_op jit(solution)/shard_map/ppermute | solution.py:261
  28.5 0.1 shard_map.54.mine
  28.6 0.1 collective-permute-start.6
  28.7 0.6 %collective-permute-start.7 = (bf16[4,128,128]{2,1,0:T(8,128)(2,1)S(1)}, bf16[4,128,128]{2,1,0:T(8,128)(2,1)S(1)}, u32[]{:S(2)}, u32[]{:S(2)}) collective-permute-start(bf16[4,128,128]{2,1,0:T(8,128)(2,1)S(1)} %get-tuple-element.41), channel_id=1, source_target_pairs={{0,4},{1,5},{2,6},{3,7},{4,0},{5,1},{6,2},{7,3},{8,12},{9,13},{10,... | collective-permute-start | bytes 393224 | tf_op jit(solution)/shard_map/ppermute | solution.py:261
  29.3 1.9 %collective-permute-start.8 = (bf16[4,128,128]{2,1,0:T(8,128)(2,1)S(1)}, bf16[4,128,128]{2,1,0:T(8,128)(2,1)S(1)}, u32[]{:S(2)}, u32[]{:S(2)}) collective-permute-start(bf16[4,128,128]{2,1,0:T(8,128)(2,1)S(1)} %get-tuple-element.42), channel_id=1, source_target_pairs={{0,2},{1,3},{2,0},{3,1},{4,6},{5,7},{6,4},{7,5},{8,10},{9,11},{10,... | collective-permute-start | bytes 393224 | tf_op jit(solution)/shard_map/ppermute | solution.py:261
  31.2 1.0 %collective-permute-start.9 = (bf16[4,128,128]{2,1,0:T(8,128)(2,1)S(1)}, bf16[4,128,128]{2,1,0:T(8,128)(2,1)S(1)}, u32[]{:S(2)}, u32[]{:S(2)}) collective-permute-start(bf16[4,128,128]{2,1,0:T(8,128)(2,1)S(1)} %get-tuple-element.43), channel_id=1, source_target_pairs={{0,6},{1,7},{2,4},{3,5},{4,2},{5,3},{6,0},{7,1},{8,14},{9,15},{10,... | collective-permute-start | bytes 393224 | tf_op jit(solution)/shard_map/ppermute | solution.py:261
  32.2 0.0 collective-permute-done.6.theirs
  32.2 0.4 shard_map.55
  32.6 0.0 copy-start.2
  32.6 2.0 %collective-permute-done.7.refs_1_ = bf16[4,128,128]{2,1,0:T(8,128)(2,1)S(1)} collective-permute-done((bf16[4,128,128]{2,1,0:T(8,128)(2,1)S(1)}, bf16[4,128,128]{2,1,0:T(8,128)(2,1)S(1)}, u32[]{:S(2)}, u32[]{:S(2)}) %collective-permute-start.7) | collective-permute-done | bytes 131104 | tf_op jit(solution)/shard_map/ppermute | solution.py:261
  34.6 1.0 %collective-permute-done.8.refs_2_ = bf16[4,128,128]{2,1,0:T(8,128)(2,1)S(1)} collective-permute-done((bf16[4,128,128]{2,1,0:T(8,128)(2,1)S(1)}, bf16[4,128,128]{2,1,0:T(8,128)(2,1)S(1)}, u32[]{:S(2)}, u32[]{:S(2)}) %collective-permute-start.8) | collective-permute-done | bytes 131104 | tf_op jit(solution)/shard_map/ppermute | solution.py:261
  35.6 3.0 %collective-permute-done.9.refs_3_ = bf16[4,128,128]{2,1,0:T(8,128)(2,1)S(1)} collective-permute-done((bf16[4,128,128]{2,1,0:T(8,128)(2,1)S(1)}, bf16[4,128,128]{2,1,0:T(8,128)(2,1)S(1)}, u32[]{:S(2)}, u32[]{:S(2)}) %collective-permute-start.9) | collective-permute-done | bytes 131104 | tf_op jit(solution)/shard_map/ppermute | solution.py:261
  38.6 1.4 %shard_map.56.refs_2_ = bf16[4,128,128]{2,1,0:T(8,128)(2,1)S(1)} custom-call(bf16[512,1024]{1,0:T(8,128)(2,1)S(1)} %get-tuple-element.38.system, bf16[512,512]{1,0:T(8,128)(2,1)S(1)} %get-tuple-element.39.rough, f32[512,128]{1,0:T(8,128)S(1)} %get-tuple-element.40.inverse, bf16[4,128,128]{2,1,0:T(8,128)(2,1)S(1)} %get-tuple-element.37.refs_4_.refs_0_, ...), custom_call_target="tpu_custom_call" | custom-call | flops 805306368 | bytes 2097152 | tf_op jit(solution)/shard_map/pallas_call | solution.py:349
  40.0 0.1 collective-permute-start.15
  40.1 1.4 %shard_map.47.order_only.refs_0_ = bf16[768,256]{1,0:T(8,128)(2,1)S(1)} custom-call(bf16[4,6,24,128]{3,2,1,0:T(8,128)(2,1)S(1)} %broadcast_in_dim.2.mask, bf16[4,6,24,128,128]{4,3,2,1,0:T(8,128)(2,1)S(1)} %copy-done, bf16[3072,256]{1,0:T(8,128)(2,1)S(1)} %copy-done.2), custom_call_target="tpu_custom_call" | custom-call | flops 1207959552 | bytes 6291456 | tf_op jit(solution)/shard_map/pallas_call | solution.py:319
  41.5 1.5 %shard_map.48 = (bf16[768,512]{1,0:T(8,128)(2,1)S(1)}, bf16[768,512]{1,0:T(8,128)(2,1)S(1)}, bf16[768,512]{1,0:T(8,128)(2,1)S(1)}, bf16[768,512]{1,0:T(8,128)(2,1)S(1)}) custom-call(s32[4,4]{1,0:T(4,128)S(1)} %copy-done.4, s32[6,4,24]{2,1,0:T(4,128)S(1)} %bitcast.2, bf16[4,6,24,128,128]{4,3,2,1,0:T(8,128)(2,1)S(1)} %copy-done, ...), custom_call_target="tpu_custom_call" | custom-call | bytes 6291456 | tf_op jit(solution)/shard_map/pallas_call | solution.py:344
  42.9 1.9 %collective-permute-start.14 = (bf16[4,128,128]{2,1,0:T(8,128)(2,1)S(1)}, bf16[4,128,128]{2,1,0:T(8,128)(2,1)S(1)}, u32[]{:S(2)}, u32[]{:S(2)}) collective-permute-start(bf16[4,128,128]{2,1,0:T(8,128)(2,1)S(1)} %shard_map.56.refs_2_), channel_id=1, source_target_pairs={{0,6},{1,7},{2,4},{3,5},{4,2},{5,3},{6,0},{7,1},{8,14},{9,15},{10,... | collective-permute-start | bytes 393224 | tf_op jit(solution)/shard_map/ppermute | solution.py:261
  44.9 1.4 %shard_map.58.refs_0_ = bf16[768,256]{1,0:T(8,128)(2,1)S(1)} custom-call(bf16[4,6,24,128]{3,2,1,0:T(8,128)(2,1)S(1)} %broadcast_in_dim.2.mask, bf16[4,6,24,128,128]{4,3,2,1,0:T(8,128)(2,1)S(1)} %copy-done, bf16[3072,256]{1,0:T(8,128)(2,1)S(1)} %copy-done.2), custom_call_target="tpu_custom_call" | custom-call | flops 1207959552 | bytes 6291456 | tf_op jit(solution)/shard_map/pallas_call | solution.py:319
  46.3 1.4 %collective-permute-start.10 = (bf16[4,128,128]{2,1,0:T(8,128)(2,1)S(1)}, bf16[4,128,128]{2,1,0:T(8,128)(2,1)S(1)}, u32[]{:S(2)}, u32[]{:S(2)}) collective-permute-start(bf16[4,128,128]{2,1,0:T(8,128)(2,1)S(1)} %shard_map.56.refs_2_), channel_id=1, source_target_pairs={{0,4},{1,5},{2,6},{3,7},{4,0},{5,1},{6,2},{7,3},{8,12},{9,13},{10,... | collective-permute-start | bytes 393224 | tf_op jit(solution)/shard_map/ppermute | solution.py:261
  47.7 0.3 collective-permute-start.12
  48.0 1.1 %shard_map.59.refs_4_ = bf16[4,768,256]{2,1,0:T(8,128)(2,1)} custom-call(bf16[768,256]{1,0:T(8,128)(2,1)S(1)} %shard_map.58.refs_0_, bf16[768,512]{1,0:T(8,128)(2,1)S(1)} %get-tuple-element.46.refs_1_, bf16[4,128,128]{2,1,0:T(8,128)(2,1)S(1)} %shard_map.56.refs_2_, bf16[4,128,128]{2,1,0:T(8,128)(2,1)S(1)} %collective-permute-done.15.refs_3_), custom_call_target="tpu_custom_call" | custom-call | flops 201326592 | bytes 2097152 | tf_op jit(solution)/shard_map/pallas_call | solution.py:367
  49.1 0.8 %collective-permute-done.14.refs_2_ = bf16[4,128,128]{2,1,0:T(8,128)(2,1)S(1)} collective-permute-done((bf16[4,128,128]{2,1,0:T(8,128)(2,1)S(1)}, bf16[4,128,128]{2,1,0:T(8,128)(2,1)S(1)}, u32[]{:S(2)}, u32[]{:S(2)}) %collective-permute-start.14) | collective-permute-done | bytes 131104 | tf_op jit(solution)/shard_map/ppermute | solution.py:261
  49.9 0.0 collective-permute-start.16
  49.9 1.4 %shard_map.46.refs_0_ = bf16[768,256]{1,0:T(8,128)(2,1)S(1)} custom-call(bf16[4,6,24,128]{3,2,1,0:T(8,128)(2,1)S(1)} %broadcast_in_dim.2.mask, bf16[4,6,24,128,128]{4,3,2,1,0:T(8,128)(2,1)S(1)} %copy-done, bf16[3072,256]{1,0:T(8,128)(2,1)S(1)} %copy-done.2), custom_call_target="tpu_custom_call" | custom-call | flops 1207959552 | bytes 6291456 | tf_op jit(solution)/shard_map/pallas_call | solution.py:319
  51.3 1.3 %collective-permute-done.10.refs_2_ = bf16[4,128,128]{2,1,0:T(8,128)(2,1)S(1)} collective-permute-done((bf16[4,128,128]{2,1,0:T(8,128)(2,1)S(1)}, bf16[4,128,128]{2,1,0:T(8,128)(2,1)S(1)}, u32[]{:S(2)}, u32[]{:S(2)}) %collective-permute-start.10) | collective-permute-done | bytes 131104 | tf_op jit(solution)/shard_map/ppermute | solution.py:261
  52.6 0.0 collective-permute-start.11
  52.6 0.4 collective-permute-done.12.refs_6_
  53.0 0.1 collective-permute-start.13
  53.1 1.4 %shard_map.57.refs_4_ = bf16[768,256]{1,0:T(8,128)(2,1)S(1)} custom-call(bf16[4,6,24,128]{3,2,1,0:T(8,128)(2,1)S(1)} %broadcast_in_dim.2.mask, bf16[4,6,24,128,128]{4,3,2,1,0:T(8,128)(2,1)S(1)} %copy-done, bf16[3072,256]{1,0:T(8,128)(2,1)S(1)} %copy-done.2), custom_call_target="tpu_custom_call" | custom-call | flops 1207959552 | bytes 6291456 | tf_op jit(solution)/shard_map/pallas_call | solution.py:319
  54.5 0.0 collective-permute-done.16.refs_3_
  54.5 1.1 %shard_map.60.refs_8_ = bf16[4,768,256]{2,1,0:T(8,128)(2,1)} custom-call(bf16[768,256]{1,0:T(8,128)(2,1)S(1)} %shard_map.47.order_only.refs_0_, bf16[768,512]{1,0:T(8,128)(2,1)S(1)} %get-tuple-element.45.refs_1_, bf16[4,128,128]{2,1,0:T(8,128)(2,1)S(1)} %collective-permute-done.14.refs_2_, ...), custom_call_target="tpu_custom_call", output_to_operand_aliasing={{}: (4, {})} | custom-call | flops 201326592 | bytes 2097152 | tf_op jit(solution)/shard_map/pallas_call | solution.py:367
  55.7 1.3 %shard_map.61 = bf16[4,768,256]{2,1,0:T(8,128)(2,1)} custom-call(bf16[768,256]{1,0:T(8,128)(2,1)S(1)} %shard_map.46.refs_0_, bf16[768,512]{1,0:T(8,128)(2,1)S(1)} %get-tuple-element.27.refs_1_, bf16[4,128,128]{2,1,0:T(8,128)(2,1)S(1)} %collective-permute-done.10.refs_2_, ...), custom_call_target="tpu_custom_call", output_to_operand_aliasing={{}: (8, {})} | custom-call | flops 402653184 | bytes 4194304 | tf_op jit(solution)/shard_map/pallas_call | solution.py:367
  (16 shorter events, 0.1 us)
Async XLA Ops:
  0.0 3.2 %copy-start.4 = (s32[4,4]{1,0:T(4,128)S(1)}, s32[4,4]{1,0:T(4,128)}, u32[]{:S(2)}) copy-start(s32[4,4]{1,0:T(4,128)} %shared.5) | copy-start | bytes 196
  0.0 3.3 %copy-start.3 = (s32[4,6,24]{2,0,1:T(4,128)S(1)}, s32[4,6,24]{2,0,1:T(4,128)}, u32[]{:S(2)}) copy-start(s32[4,6,24]{2,0,1:T(4,128)} %param.5) | copy-start | bytes 6916
  0.0 6.6 %copy-start = (bf16[4,6,24,128,128]{4,3,2,1,0:T(8,128)(2,1)S(1)}, bf16[4,6,24,128,128]{4,3,2,1,0:T(8,128)(2,1)}, u32[]{:S(2)}) copy-start(bf16[4,6,24,128,128]{4,3,2,1,0:T(8,128)(2,1)} %blocks.13) | copy-start | bytes 56623108
  2.6 13.3 %collective-permute-start = (bf16[3,2,128,512]{3,2,1,0:T(8,128)(2,1)S(1)}, bf16[3,2,128,512]{3,2,1,0:T(8,128)(2,1)S(1)}, u32[]{:S(2)}, u32[]{:S(2)}) collective-permute-start(bf16[3,2,128,512]{3,2,1,0:T(8,128)(2,1)S(1)} %get-tuple-element.29), channel_id=1, source_target_pairs={{0,1},{1,0},{2,3},{3,2},{4,5},{5,4},{6,7},{7,6},{8,9},{9,8},{10,11... | collective-permute-start | bytes 2359304 | tf_op jit(solution)/shard_map/ppermute | solution.py:253
  2.9 7.8 %collective-permute-start.3 = (bf16[1,2,128,512]{3,2,1,0:T(8,128)(2,1)S(1)}, bf16[1,2,128,512]{3,2,1,0:T(8,128)(2,1)S(1)}, u32[]{:S(2)}, u32[]{:S(2)}) collective-permute-start(bf16[1,2,128,512]{3,2,1,0:T(8,128)(2,1)S(1)} %get-tuple-element.34), channel_id=1, source_target_pairs={{0,1},{1,0},{2,3},{3,2},{4,5},{5,4},{6,7},{7,6},{8,9},{9,8},{10,11... | collective-permute-start | bytes 786440 | tf_op jit(solution)/shard_map/ppermute | solution.py:253
  6.6 1.4 %copy-start.1 = (bf16[3072,256]{1,0:T(8,128)(2,1)S(1)}, bf16[3072,256]{1,0:T(8,128)(2,1)}, u32[]{:S(2)}) copy-start(bf16[3072,256]{1,0:T(8,128)(2,1)} %sketch.9) | copy-start | bytes 4718596
  10.6 6.1 %collective-permute-start.5 = (bf16[4,4,128,128]{3,2,1,0:T(8,128)(2,1)S(1)}, bf16[4,4,128,128]{3,2,1,0:T(8,128)(2,1)S(1)}, u32[]{:S(2)}, u32[]{:S(2)}) collective-permute-start(bf16[4,4,128,128]{3,2,1,0:T(8,128)(2,1)S(1)} %get-tuple-element.36), channel_id=1, source_target_pairs={{0,1},{1,0},{2,3},{3,2},{4,5},{5,4},{6,7},{7,6},{8,9},{9,8},{10,11... | collective-permute-start | bytes 1572872 | tf_op jit(solution)/shard_map/ppermute | solution.py:253
  10.8 12.4 %collective-permute-start.4 = (bf16[2,128,512]{2,1,0:T(8,128)(2,1)S(1)}, bf16[2,128,512]{2,1,0:T(8,128)(2,1)S(1)}, u32[]{:S(2)}, u32[]{:S(2)}) collective-permute-start(bf16[2,128,512]{2,1,0:T(8,128)(2,1)S(1)} %shard_map.51), channel_id=1, source_target_pairs={{0,6},{1,7},{2,4},{3,5},{4,2},{5,3},{6,0},{7,1},{8,14},{9,15},{10,... | collective-permute-start | bytes 786440 | tf_op jit(solution)/shard_map/ppermute | solution.py:261
  16.1 12.5 %collective-permute-start.1 = (bf16[2,128,512]{2,1,0:T(8,128)(2,1)S(1)}, bf16[2,128,512]{2,1,0:T(8,128)(2,1)S(1)}, u32[]{:S(2)}, u32[]{:S(2)}) collective-permute-start(bf16[2,128,512]{2,1,0:T(8,128)(2,1)S(1)} %get-tuple-element.31), channel_id=1, source_target_pairs={{0,4},{1,5},{2,6},{3,7},{4,0},{5,1},{6,2},{7,3},{8,12},{9,13},{10,... | collective-permute-start | bytes 786440 | tf_op jit(solution)/shard_map/ppermute | solution.py:261
  16.1 12.4 %collective-permute-start.2 = (bf16[2,128,512]{2,1,0:T(8,128)(2,1)S(1)}, bf16[2,128,512]{2,1,0:T(8,128)(2,1)S(1)}, u32[]{:S(2)}, u32[]{:S(2)}) collective-permute-start(bf16[2,128,512]{2,1,0:T(8,128)(2,1)S(1)} %get-tuple-element.32), channel_id=1, source_target_pairs={{0,2},{1,3},{2,0},{3,1},{4,6},{5,7},{6,4},{7,5},{8,10},{9,11},{10,... | collective-permute-start | bytes 786440 | tf_op jit(solution)/shard_map/ppermute | solution.py:261
  28.6 3.6 %collective-permute-start.6 = (bf16[2,2,128,512]{3,2,1,0:T(8,128)(2,1)S(1)}, bf16[2,2,128,512]{3,2,1,0:T(8,128)(2,1)S(1)}, u32[]{:S(2)}, u32[]{:S(2)}) collective-permute-start(bf16[2,2,128,512]{3,2,1,0:T(8,128)(2,1)S(1)} %shard_map.54.mine), channel_id=1, source_target_pairs={{0,1},{1,0},{2,3},{3,2},{4,5},{5,4},{6,7},{7,6},{8,9},{9,8},{10,11... | collective-permute-start | bytes 1572872 | tf_op jit(solution)/shard_map/ppermute | solution.py:253
  28.7 5.9 %collective-permute-start.7 = (bf16[4,128,128]{2,1,0:T(8,128)(2,1)S(1)}, bf16[4,128,128]{2,1,0:T(8,128)(2,1)S(1)}, u32[]{:S(2)}, u32[]{:S(2)}) collective-permute-start(bf16[4,128,128]{2,1,0:T(8,128)(2,1)S(1)} %get-tuple-element.41), channel_id=1, source_target_pairs={{0,4},{1,5},{2,6},{3,7},{4,0},{5,1},{6,2},{7,3},{8,12},{9,13},{10,... | collective-permute-start | bytes 393224 | tf_op jit(solution)/shard_map/ppermute | solution.py:261
  29.3 6.3 %collective-permute-start.8 = (bf16[4,128,128]{2,1,0:T(8,128)(2,1)S(1)}, bf16[4,128,128]{2,1,0:T(8,128)(2,1)S(1)}, u32[]{:S(2)}, u32[]{:S(2)}) collective-permute-start(bf16[4,128,128]{2,1,0:T(8,128)(2,1)S(1)} %get-tuple-element.42), channel_id=1, source_target_pairs={{0,2},{1,3},{2,0},{3,1},{4,6},{5,7},{6,4},{7,5},{8,10},{9,11},{10,... | collective-permute-start | bytes 393224 | tf_op jit(solution)/shard_map/ppermute | solution.py:261
  31.2 7.4 %collective-permute-start.9 = (bf16[4,128,128]{2,1,0:T(8,128)(2,1)S(1)}, bf16[4,128,128]{2,1,0:T(8,128)(2,1)S(1)}, u32[]{:S(2)}, u32[]{:S(2)}) collective-permute-start(bf16[4,128,128]{2,1,0:T(8,128)(2,1)S(1)} %get-tuple-element.43), channel_id=1, source_target_pairs={{0,6},{1,7},{2,4},{3,5},{4,2},{5,3},{6,0},{7,1},{8,14},{9,15},{10,... | collective-permute-start | bytes 393224 | tf_op jit(solution)/shard_map/ppermute | solution.py:261
  32.6 7.5 %copy-start.2 = (bf16[3072,256]{1,0:T(8,128)(2,1)S(1)}, bf16[3072,256]{1,0:T(8,128)(2,1)}, u32[]{:S(2)}) copy-start(bf16[3072,256]{1,0:T(8,128)(2,1)} %sketch.9) | copy-start | bytes 4718596
  40.0 8.0 %collective-permute-start.15 = (bf16[4,128,128]{2,1,0:T(8,128)(2,1)S(1)}, bf16[4,128,128]{2,1,0:T(8,128)(2,1)S(1)}, u32[]{:S(2)}, u32[]{:S(2)}) collective-permute-start(bf16[4,128,128]{2,1,0:T(8,128)(2,1)S(1)} %shard_map.56.refs_2_), channel_id=1, source_target_pairs={{0,1},{1,0},{2,3},{3,2},{4,5},{5,4},{6,7},{7,6},{8,9},{9,8},{10,11... | collective-permute-start | bytes 393224 | tf_op jit(solution)/shard_map/ppermute | solution.py:253
  42.9 6.9 %collective-permute-start.14 = (bf16[4,128,128]{2,1,0:T(8,128)(2,1)S(1)}, bf16[4,128,128]{2,1,0:T(8,128)(2,1)S(1)}, u32[]{:S(2)}, u32[]{:S(2)}) collective-permute-start(bf16[4,128,128]{2,1,0:T(8,128)(2,1)S(1)} %shard_map.56.refs_2_), channel_id=1, source_target_pairs={{0,6},{1,7},{2,4},{3,5},{4,2},{5,3},{6,0},{7,1},{8,14},{9,15},{10,... | collective-permute-start | bytes 393224 | tf_op jit(solution)/shard_map/ppermute | solution.py:261
  46.3 6.3 %collective-permute-start.10 = (bf16[4,128,128]{2,1,0:T(8,128)(2,1)S(1)}, bf16[4,128,128]{2,1,0:T(8,128)(2,1)S(1)}, u32[]{:S(2)}, u32[]{:S(2)}) collective-permute-start(bf16[4,128,128]{2,1,0:T(8,128)(2,1)S(1)} %shard_map.56.refs_2_), channel_id=1, source_target_pairs={{0,4},{1,5},{2,6},{3,7},{4,0},{5,1},{6,2},{7,3},{8,12},{9,13},{10,... | collective-permute-start | bytes 393224 | tf_op jit(solution)/shard_map/ppermute | solution.py:261
  47.7 5.3 %collective-permute-start.12 = (bf16[4,128,128]{2,1,0:T(8,128)(2,1)S(1)}, bf16[4,128,128]{2,1,0:T(8,128)(2,1)S(1)}, u32[]{:S(2)}, u32[]{:S(2)}) collective-permute-start(bf16[4,128,128]{2,1,0:T(8,128)(2,1)S(1)} %shard_map.56.refs_2_), channel_id=1, source_target_pairs={{0,2},{1,3},{2,0},{3,1},{4,6},{5,7},{6,4},{7,5},{8,10},{9,11},{10,... | collective-permute-start | bytes 393224 | tf_op jit(solution)/shard_map/ppermute | solution.py:261
  49.9 4.7 %collective-permute-start.16 = (bf16[4,128,128]{2,1,0:T(8,128)(2,1)S(1)}, bf16[4,128,128]{2,1,0:T(8,128)(2,1)S(1)}, u32[]{:S(2)}, u32[]{:S(2)}) collective-permute-start(bf16[4,128,128]{2,1,0:T(8,128)(2,1)S(1)} %collective-permute-done.14.refs_2_), channel_id=1, source_target_pairs={{0,1},{1,0},{2,3},{3,2},{4,5},{5,4},{6,7},{7,6},{8,9},{9,8},{10,11... | collective-permute-start | bytes 393224 | tf_op jit(solution)/shard_map/ppermute | solution.py:253
  52.6 3.1 %collective-permute-start.11 = (bf16[4,128,128]{2,1,0:T(8,128)(2,1)S(1)}, bf16[4,128,128]{2,1,0:T(8,128)(2,1)S(1)}, u32[]{:S(2)}, u32[]{:S(2)}) collective-permute-start(bf16[4,128,128]{2,1,0:T(8,128)(2,1)S(1)} %collective-permute-done.10.refs_2_), channel_id=1, source_target_pairs={{0,1},{1,0},{2,3},{3,2},{4,5},{5,4},{6,7},{7,6},{8,9},{9,8},{10,11... | collective-permute-start | bytes 393224 | tf_op jit(solution)/shard_map/ppermute | solution.py:253
  53.0 2.7 %collective-permute-start.13 = (bf16[4,128,128]{2,1,0:T(8,128)(2,1)S(1)}, bf16[4,128,128]{2,1,0:T(8,128)(2,1)S(1)}, u32[]{:S(2)}, u32[]{:S(2)}) collective-permute-start(bf16[4,128,128]{2,1,0:T(8,128)(2,1)S(1)} %collective-permute-done.12.refs_6_), channel_id=1, source_target_pairs={{0,1},{1,0},{2,3},{3,2},{4,5},{5,4},{6,7},{7,6},{8,9},{9,8},{10,11... | collective-permute-start | bytes 393224 | tf_op jit(solution)/shard_map/ppermute | solution.py:253
